TPU v7x, 128 devices: a whole 4x4x4 slice. The times are simulated.
128 devices in a mesh: space: 64 (over x, y, z), level: 2 (over core).
Axes of the slice: x: 4, y: 4, z: 4, core: 2. Of those that a mesh axis runs over, the one named last changes fastest.
Arguments:
- multipole_fine: bfloat16 [512, 16, 16, 152], P('space'), may hold values from -6 to 6
- multipole_mid: bfloat16 [256, 8, 8, 152], P('space'), may hold values from -6 to 6
- multipole_coarse: bfloat16 [128, 4, 4, 152], P('space'), may hold values from -6 to 6
- multipole_top: bfloat16 [64, 2, 2, 152], P('space'), may hold values from -6 to 6
- translation_ops: bfloat16 [7, 7, 7, 152, 152], replicated, may hold values from -0.03125 to 0.03125
- upsample_ops: bfloat16 [2, 2, 2, 152, 152], replicated, may hold values from -0.5 to 0.5
Outputs:
- local_fine: float32 [512, 16, 16, 152], P('space', 'level')
All inputs are finite; a program needn't handle non-finite values.
Results may differ from a plain program's by a relative error of at most 0.0003.
Values may be sent and summed in bfloat16 or wider, within the bound.
A program may use at most 448 MiB of HBM per device.

v0:
```python
import jax
import jax.numpy as jnp
from jax import lax
from jax.sharding import PartitionSpec as P


def with_halo(value, sides, width):
    for axis, dim in sides:
        devices, length = (lax.axis_size(axis), value.shape[dim])
        up = [(i, (i + 1) % devices) for i in range(devices - 1)]
        down = [(j, i) for i, j in up]
        last = lax.slice_in_dim(value, length - width, length, axis=dim)
        initial = lax.slice_in_dim(value, 0, width, axis=dim)
        before = lax.ppermute(last, axis, up)
        after = lax.ppermute(initial, axis, down)
        value = jnp.concatenate([before, value, after], axis=dim)
    return value


def partner_2(block, axis, stride):
    count = lax.axis_size(axis)
    route = []
    for low in range(count):
        high = low | 1 << stride
        if high != low and high < count:
            route += [(low, high), (high, low)]
    return lax.ppermute(block, axis, route)


def from_behind(value, axis, by):
    devices = lax.axis_size(axis)
    pairs = [(i, i + by) for i in range(devices) if 0 <= i + by < devices]
    return lax.ppermute(value, axis, pairs)


def near_blocks(number_type):
    position = jnp.arange(7)
    inside = (position >= 2) & (position <= 4)
    center = inside[:, None, None] & inside[None, :, None] & inside[None, None, :]
    return jnp.where(center, 0.0, 1.0).astype(number_type)[:, :, :, None, None]


def parity_kernels(masked_ops, source_parity):
    channels = masked_ops.shape[-1]
    kernels = []
    for parity_x in range(2):
        for parity_y in range(2):
            for parity_z in range(2):
                window = masked_ops[
                    1 - parity_x : 7 - parity_x,
                    1 - parity_y : 7 - parity_y,
                    1 - parity_z : 7 - parity_z,
                ]
                window = window.reshape(3, 2, 3, 2, 3, 2, channels, channels)
                window = lax.dynamic_slice_in_dim(window, source_parity, 1, 3)
                window = window.transpose(0, 2, 4, 1, 3, 5, 6, 7)
                kernels.append(window.reshape(-1, channels))
    return kernels


def parity_split(extended):
    size_x, size_y, size_z, channels = extended.shape
    grouped = extended.reshape(size_x // 2, 2, size_y // 2, 2, size_z // 2, 2, channels)
    return grouped.transpose(0, 2, 4, 1, 3, 5, 6)


def pad_sides(field):
    return jnp.pad(field, ((0, 0), (2, 2), (2, 2), (0, 0)))


def far_field(extended, kernels, source_parity, count_y, y_start):
    parity_grid = parity_split(extended)
    parity_grid = lax.dynamic_slice_in_dim(parity_grid, source_parity, 1, 4)
    count_x = parity_grid.shape[0] - 2
    count_z = parity_grid.shape[2] - 2
    channels = parity_grid.shape[-1]
    sections = []
    for step_x in range(3):
        for step_y in range(3):
            for step_z in range(3):
                section = lax.dynamic_slice_in_dim(parity_grid, y_start + step_y, count_y, 1)
                sections.append(section[step_x : step_x + count_x, :, step_z : step_z + count_z])
    stacked = jnp.stack(sections, axis=3).reshape(count_x * count_y * count_z, -1)
    results = [jnp.dot(stacked, kernel, preferred_element_type=jnp.float32) for kernel in kernels]
    joined = jnp.stack(results, axis=1).reshape(count_x, count_y, count_z, 2, 2, 2, channels)
    joined = joined.transpose(0, 3, 1, 4, 2, 5, 6)
    return joined.reshape(2 * count_x, 2 * count_y, 2 * count_z, channels)


def level_far(multipole, kernels, source_parity):
    with_rims = with_halo(multipole, (("space", 0),), 2)
    extended = pad_sides(with_rims)
    parents_y = multipole.shape[1] // 2
    return far_field(extended, kernels, source_parity, parents_y, 0)


def top_sources(multipole_top):
    column = lax.axis_index("space")
    is_even = column % 2 == 0
    partner = partner_2(multipole_top, "space", 0)
    with_next = jnp.concatenate([multipole_top, partner], axis=0)
    with_prev = jnp.concatenate([partner, multipole_top], axis=0)
    pair_block = jnp.where(is_even, with_next, with_prev)
    neighbours = []
    for distance in (2, -2):
        neighbours.append(from_behind(pair_block, "space", distance))
    sources = jnp.concatenate([neighbours[0], pair_block, neighbours[1]], axis=0)
    return pad_sides(sources)


def upsample(parent, upsample_ops):
    children = jnp.einsum(
        "xyzi,abcio->xaybzco",
        parent,
        upsample_ops.astype(jnp.float32),
        precision=lax.Precision.HIGHEST,
        preferred_element_type=jnp.float32,
    )
    size_x, size_y, size_z, channels = parent.shape
    return children.reshape(2 * size_x, 2 * size_y, 2 * size_z, channels)


def sum_levels(partial_value):
    return lax.psum_scatter(partial_value, "level", scatter_dimension=1, tiled=True)


def shards(
    multipole_fine, multipole_mid, multipole_coarse, multipole_top, translation_ops, upsample_ops
):
    masked_ops = translation_ops * near_blocks(translation_ops.dtype)
    core_index = lax.axis_index("level")
    column = lax.axis_index("space")
    top_extended = top_sources(multipole_top)
    top_count = multipole_top.shape[1] // 2
    finer_levels = (multipole_coarse, multipole_mid, multipole_fine)
    kernels = parity_kernels(masked_ops, core_index)
    top_far = far_field(top_extended, kernels, core_index, top_count, 0)
    local_exp = sum_levels(lax.dynamic_slice_in_dim(top_far, column % 2, 1, 0))
    for multipole in finer_levels:
        local_exp = sum_levels(level_far(multipole, kernels, core_index)) + upsample(
            local_exp, upsample_ops
        )
    return local_exp


def solution(mesh):
    placed = (
        P("space", None, None, None),
        P("space", None, None, None),
        P("space", None, None, None),
        P("space", None, None, None),
        P(),
        P(),
    )
    return jax.shard_map(
        shards,
        mesh=mesh,
        in_specs=placed,
        out_specs=P("space", "level", None, None),
        check_vma=False,
    )
```

profile of v0, /device:TPU:6, one launch (start us, length us, event | category | flops | bytes accessed | tf_op | source)
XLA Modules:
  0.0 717.3 jit_solution(11606573404764910049)
XLA Ops:
  6.5 8.8 %collective-permute-start.5 = (bf16[2,4,4,152]{3,2,1,0:T(4,128)(2,1)}, bf16[2,4,4,152]{3,2,1,0:T(4,128)(2,1)}, u32[]{:S(2)}, u32[]{:S(2)}) collective-permute-start(bf16[2,4,4,152]{3,2,1,0:T(4,128)(2,1)} %param.8), channel_id=1, source_target_pairs={{2,0},{4,2},{6,4},{8,6},{10,8},{12,10},{14,12},{16,14},{18,16},{20... | collective-permute-start | bytes 29192 | tf_op jit(solution)/shard_map/ppermute | solution.py:15
  27.2 18.6 %broadcast_multiply_fusion = bf16[7,7,7,152,152]{4,3,2,1,0:T(8,128)(2,1)} fusion(bf16[7,7,7,152,152]{4,3,2,1,0:T(8,128)(2,1)} %param.10, bf16[7,7,7]{2,1,0:T(8,128)(2,1)S(1)} %select_convert_fusion), kind=kLoop, calls=%fused_computation | loop fusion | flops 7924672 | bytes 31699374 | tf_op jit(solution)/shard_map/mul | solution.py:130
  45.8 86.0 %fusion.84 = (bf16[6,6,6,152,152]{4,3,2,1,0:T(8,128)(2,1)}, bf16[6,6,6,152,152]{4,3,2,1,0:T(8,128)(2,1)}, bf16[6,6,6,152,152]{4,3,2,1,0:T(8,128)(2,1)}, bf16[6,6...) fusion(bf16[7,7,7,152,152]{4,3,2,1,0:T(8,128)(2,1)} %broadcast_, ...), kind=kLoop, calls=%fused_computation.358 | loop fusion | bytes 159694848 | tf_op jit(solution)/shard_map/slice | solution.py:49
  131.9 13.2 %constant_dynamic-slice_fusion.9 = (bf16[3,2,3,1,3,2,152,152]{7,6,5,4,3,2,1,0:T(8,128)(2,1)}, bf16[3,2,3,1,3,2,152,152]{7,6,5,4,3,2,1,0:T(8,128)(2,1)}) fusion(bf16[3,2,3,2,3,2,152,152]{7,6,5,4,3,2,1,0:T(8,128)(2,1)} %bitcast.978, s32[]{:T(128)S(6)} %select_n.42, bf16[3,2,3,2,3,2,152,152]{7,6,5,4,3,2,1,0:T(8,128)(2,1)} %bitcast.979), kind=kLoop, calls=%fused_computation.321 | loop fusion | bytes 19961860 | tf_op jit(solution)/shard_map/dynamic_slice | solution.py:55
  148.5 11.7 %constant_dynamic-slice_fusion.7 = (bf16[3,2,3,1,3,2,152,152]{7,6,5,4,3,2,1,0:T(8,128)(2,1)}, bf16[3,2,3,1,3,2,152,152]{7,6,5,4,3,2,1,0:T(8,128)(2,1)}) fusion(bf16[3,2,3,2,3,2,152,152]{7,6,5,4,3,2,1,0:T(8,128)(2,1)S(1)} %bitcast.976, s32[]{:T(128)S(6)} %select_n.42, bf16[3,2,3,2,3,2,152,152]{7,6,5,4,3,2,1,0:T(8,128)(2,1)} %bitcast.977), kind=kLoop, calls=%fused_computation.319 | loop fusion | bytes 19961860 | tf_op jit(solution)/shard_map/dynamic_slice | solution.py:55
  160.2 13.2 %constant_dynamic-slice_fusion.5 = (bf16[3,2,3,1,3,2,152,152]{7,6,5,4,3,2,1,0:T(8,128)(2,1)}, bf16[3,2,3,1,3,2,152,152]{7,6,5,4,3,2,1,0:T(8,128)(2,1)}) fusion(bf16[3,2,3,2,3,2,152,152]{7,6,5,4,3,2,1,0:T(8,128)(2,1)} %bitcast.972, s32[]{:T(128)S(6)} %select_n.42, bf16[3,2,3,2,3,2,152,152]{7,6,5,4,3,2,1,0:T(8,128)(2,1)} %bitcast.973), kind=kLoop, calls=%fused_computation.317 | loop fusion | bytes 19961860 | tf_op jit(solution)/shard_map/dynamic_slice | solution.py:55
  194.1 19.4 %copy.625 = bf16[3,2,3,1,3,2,152,152]{6,5,1,4,2,0,7,3:T(2,128)(2,1)} copy(bf16[3,2,3,1,3,2,152,152]{7,6,5,4,3,2,1,0:T(8,128)(2,1)} %get-tuple-element.28) | data formatting | bytes 9980928
  213.5 18.3 %reshape.194 = bf16[16416,152]{0,1:T(8,128)(2,1)} reshape(bf16[3,3,3,2,1,2,152,152]{6,5,3,2,1,0,7,4:T(2,128)(2,1)} %bitcast.980) | data formatting | bytes 9980928 | tf_op jit(solution)/shard_map/reshape | solution.py:57
  231.8 19.4 %copy.626 = bf16[3,2,3,1,3,2,152,152]{6,5,1,4,2,0,7,3:T(2,128)(2,1)} copy(bf16[3,2,3,1,3,2,152,152]{7,6,5,4,3,2,1,0:T(8,128)(2,1)} %get-tuple-element.27) | data formatting | bytes 9980928
  251.2 18.3 %reshape.196 = bf16[16416,152]{0,1:T(8,128)(2,1)} reshape(bf16[3,3,3,2,1,2,152,152]{6,5,3,2,1,0,7,4:T(2,128)(2,1)} %bitcast.981) | data formatting | bytes 9980928 | tf_op jit(solution)/shard_map/reshape | solution.py:57
  269.5 19.4 %copy.627 = bf16[3,2,3,1,3,2,152,152]{6,5,1,4,2,0,7,3:T(2,128)(2,1)} copy(bf16[3,2,3,1,3,2,152,152]{7,6,5,4,3,2,1,0:T(8,128)(2,1)} %get-tuple-element.26) | data formatting | bytes 9980928
  288.9 18.3 %reshape.198 = bf16[16416,152]{0,1:T(8,128)(2,1)} reshape(bf16[3,3,3,2,1,2,152,152]{6,5,3,2,1,0,7,4:T(2,128)(2,1)} %bitcast.982) | data formatting | bytes 9980928 | tf_op jit(solution)/shard_map/reshape | solution.py:57
  307.1 19.4 %copy.628 = bf16[3,2,3,1,3,2,152,152]{6,5,1,4,2,0,7,3:T(2,128)(2,1)} copy(bf16[3,2,3,1,3,2,152,152]{7,6,5,4,3,2,1,0:T(8,128)(2,1)} %get-tuple-element.25) | data formatting | bytes 9980928
  326.6 18.3 %reshape.200 = bf16[16416,152]{0,1:T(8,128)(2,1)} reshape(bf16[3,3,3,2,1,2,152,152]{6,5,3,2,1,0,7,4:T(2,128)(2,1)} %bitcast.983) | data formatting | bytes 9980928 | tf_op jit(solution)/shard_map/reshape | solution.py:57
  344.8 19.4 %copy.629 = bf16[3,2,3,1,3,2,152,152]{6,5,1,4,2,0,7,3:T(2,128)(2,1)} copy(bf16[3,2,3,1,3,2,152,152]{7,6,5,4,3,2,1,0:T(8,128)(2,1)} %get-tuple-element.24) | data formatting | bytes 9980928
  364.2 18.5 %reshape.202 = bf16[16416,152]{0,1:T(8,128)(2,1)} reshape(bf16[3,3,3,2,1,2,152,152]{6,5,3,2,1,0,7,4:T(2,128)(2,1)} %bitcast.984) | data formatting | bytes 9980928 | tf_op jit(solution)/shard_map/reshape | solution.py:57
  382.7 19.4 %copy.630 = bf16[3,2,3,1,3,2,152,152]{6,5,1,4,2,0,7,3:T(2,128)(2,1)} copy(bf16[3,2,3,1,3,2,152,152]{7,6,5,4,3,2,1,0:T(8,128)(2,1)} %get-tuple-element.23) | data formatting | bytes 9980928
  402.1 18.3 %reshape.204 = bf16[16416,152]{0,1:T(8,128)(2,1)} reshape(bf16[3,3,3,2,1,2,152,152]{6,5,3,2,1,0,7,4:T(2,128)(2,1)} %bitcast.985) | data formatting | bytes 9980928 | tf_op jit(solution)/shard_map/reshape | solution.py:57
  420.4 19.5 %copy.631 = bf16[3,2,3,1,3,2,152,152]{6,5,1,4,2,0,7,3:T(2,128)(2,1)} copy(bf16[3,2,3,1,3,2,152,152]{7,6,5,4,3,2,1,0:T(8,128)(2,1)} %get-tuple-element.22) | data formatting | bytes 9980928
  439.9 18.3 %reshape.206 = bf16[16416,152]{0,1:T(8,128)(2,1)} reshape(bf16[3,3,3,2,1,2,152,152]{6,5,3,2,1,0,7,4:T(2,128)(2,1)} %bitcast.986) | data formatting | bytes 9980928 | tf_op jit(solution)/shard_map/reshape | solution.py:57
  458.2 19.5 %copy.632 = bf16[3,2,3,1,3,2,152,152]{6,5,1,4,2,0,7,3:T(2,128)(2,1)} copy(bf16[3,2,3,1,3,2,152,152]{7,6,5,4,3,2,1,0:T(8,128)(2,1)} %get-tuple-element.21) | data formatting | bytes 9980928
  477.7 18.3 %reshape.208 = bf16[16416,152]{0,1:T(8,128)(2,1)} reshape(bf16[3,3,3,2,1,2,152,152]{6,5,3,2,1,0,7,4:T(2,128)(2,1)} %bitcast.987) | data formatting | bytes 9980928 | tf_op jit(solution)/shard_map/reshape | solution.py:57
  499.8 8.5 %collective-permute-start.1 = (bf16[2,16,16,152]{3,2,1,0:T(8,128)(2,1)}, bf16[2,16,16,152]{3,2,1,0:T(8,128)(2,1)S(1)}, u32[]{:S(2)}, u32[]{:S(2)}) collective-permute-start(bf16[2,16,16,152]{3,2,1,0:T(8,128)(2,1)} %get-tuple-element.16), channel_id=1, source_target_pairs={{2,0},{4,2},{6,4},{8,6},{10,8},{12,10},{14,12},{16,14},{18,16},{20... | collective-permute-start | bytes 466952 | tf_op jit(solution)/shard_map/ppermute | solution.py:15
  621.9 18.4 %reshape.192 = bf16[256,16416]{1,0:T(8,128)(2,1)} reshape(bf16[4,8,8,27,2,1,2,152]{7,6,4,3,2,1,0,5:T(2,128)(2,1)} %fusion.38) | data formatting | bytes 16809984 | tf_op jit(solution)/shard_map/reshape | solution.py:83
  (365 shorter events, 220.1 us)
Async XLA Ops:
  6.5 695.6 %copy-start = (bf16[2,2,2,152,152]{4,3,2,1,0:T(8,128)(2,1)S(1)}, bf16[2,2,2,152,152]{4,3,2,1,0:T(8,128)(2,1)}, u32[]{:S(2)}) copy-start(bf16[2,2,2,152,152]{4,3,2,1,0:T(8,128)(2,1)} %param.11) | copy-start | bytes 1108996
  6.5 697.2 %all-reduce.10.cloned.1.call-start = ((), (), s32[]{:S(2)}) async-start(), calls=%async_computation.2 | async-start | bytes 524288
  6.5 522.0 %collective-permute-start.5 = (bf16[2,4,4,152]{3,2,1,0:T(4,128)(2,1)}, bf16[2,4,4,152]{3,2,1,0:T(4,128)(2,1)}, u32[]{:S(2)}, u32[]{:S(2)}) collective-permute-start(bf16[2,4,4,152]{3,2,1,0:T(4,128)(2,1)} %param.8), channel_id=1, source_target_pairs={{2,0},{4,2},{6,4},{8,6},{10,8},{12,10},{14,12},{16,14},{18,16},{20... | collective-permute-start | bytes 29192 | tf_op jit(solution)/shard_map/ppermute | solution.py:15
  15.3 515.4 %collective-permute-start.4 = (bf16[2,4,4,152]{3,2,1,0:T(4,128)(2,1)}, bf16[2,4,4,152]{3,2,1,0:T(4,128)(2,1)}, u32[]{:S(2)}, u32[]{:S(2)}) collective-permute-start(bf16[2,4,4,152]{3,2,1,0:T(4,128)(2,1)} %param.8), channel_id=1, source_target_pairs={{0,2},{2,4},{4,6},{6,8},{8,10},{10,12},{12,14},{14,16},{16,18},{18... | collective-permute-start | bytes 29192 | tf_op jit(solution)/shard_map/ppermute | solution.py:14
  17.3 167.7 %collective-permute-start.6 = (bf16[1,2,2,152]{3,2,1,0:T(2,128)(2,1)}, bf16[1,2,2,152]{3,2,1,0:T(2,128)(2,1)}, u32[]{:S(2)}, u32[]{:S(2)}) collective-permute-start(bf16[1,2,2,152]{3,2,1,0:T(2,128)(2,1)} %param.9), channel_id=1, source_target_pairs={{0,2},{2,0},{4,6},{6,4},{8,10},{10,8},{12,14},{14,12},{16,18},{18,... | collective-permute-start | bytes 3656 | tf_op jit(solution)/shard_map/ppermute | solution.py:27
  18.9 522.9 %collective-permute-start.3 = (bf16[2,8,8,152]{3,2,1,0:T(8,128)(2,1)}, bf16[2,8,8,152]{3,2,1,0:T(8,128)(2,1)}, u32[]{:S(2)}, u32[]{:S(2)}) collective-permute-start(bf16[2,8,8,152]{3,2,1,0:T(8,128)(2,1)} %get-tuple-element.20), channel_id=1, source_target_pairs={{2,0},{4,2},{6,4},{8,6},{10,8},{12,10},{14,12},{16,14},{18,16},{20... | collective-permute-start | bytes 116744 | tf_op jit(solution)/shard_map/ppermute | solution.py:15
  131.9 16.6 %slice-start.55 = ((s8[16809984]{0:T(1024)(128)(4,1)}), s8[4194304]{0:T(1024)(128)(4,1)S(1)}, s32[]{:S(2)}) async-start(s8[16809984]{0:T(1024)(128)(4,1)} %bitcast.974), calls=%async_computation.58 | async-start | bytes 8388608
  131.9 16.6 %slice-start.56 = ((s8[16809984]{0:T(1024)(128)(4,1)}), s8[32768]{0:T(1024)(128)(4,1)S(1)}, s32[]{:S(2)}) async-start(s8[16809984]{0:T(1024)(128)(4,1)} %bitcast.974), calls=%async_computation.59 | async-start | bytes 65536
  148.5 25.0 %slice-start.47 = ((s8[16809984]{0:T(1024)(128)(4,1)}), s8[4194304]{0:T(1024)(128)(4,1)S(1)}, s32[]{:S(2)}) async-start(s8[16809984]{0:T(1024)(128)(4,1)} %bitcast.969), calls=%async_computation.50 | async-start | bytes 8388608
  148.5 25.0 %slice-start.48 = ((s8[16809984]{0:T(1024)(128)(4,1)}), s8[4194304]{0:T(1024)(128)(4,1)S(1)}, s32[]{:S(2)}) async-start(s8[16809984]{0:T(1024)(128)(4,1)} %bitcast.969), calls=%async_computation.51 | async-start | bytes 8388608
  148.5 25.0 %slice-start.49 = ((s8[16809984]{0:T(1024)(128)(4,1)}), s8[4194304]{0:T(1024)(128)(4,1)S(1)}, s32[]{:S(2)}) async-start(s8[16809984]{0:T(1024)(128)(4,1)} %bitcast.969), calls=%async_computation.52 | async-start | bytes 8388608
  160.2 15.8 %slice-start.44 = ((s8[16809984]{0:T(1024)(128)(4,1)}), s8[4194304]{0:T(1024)(128)(4,1)S(1)}, s32[]{:S(2)}) async-start(s8[16809984]{0:T(1024)(128)(4,1)} %bitcast.966), calls=%async_computation.47 | async-start | bytes 8388608
  160.2 17.0 %slice-start.45 = ((s8[16809984]{0:T(1024)(128)(4,1)}), s8[4194304]{0:T(1024)(128)(4,1)S(1)}, s32[]{:S(2)}) async-start(s8[16809984]{0:T(1024)(128)(4,1)} %bitcast.966), calls=%async_computation.48 | async-start | bytes 8388608
  160.2 17.0 %slice-start.46 = ((s8[16809984]{0:T(1024)(128)(4,1)}), s8[32768]{0:T(1024)(128)(4,1)S(1)}, s32[]{:S(2)}) async-start(s8[16809984]{0:T(1024)(128)(4,1)} %bitcast.966), calls=%async_computation.49 | async-start | bytes 65536
  160.2 18.2 %slice-start.50 = ((s8[16809984]{0:T(1024)(128)(4,1)}), s8[4194304]{0:T(1024)(128)(4,1)S(1)}, s32[]{:S(2)}) async-start(s8[16809984]{0:T(1024)(128)(4,1)} %bitcast.969), calls=%async_computation.53 | async-start | bytes 8388608
  160.2 18.2 %slice-start.51 = ((s8[16809984]{0:T(1024)(128)(4,1)}), s8[32768]{0:T(1024)(128)(4,1)S(1)}, s32[]{:S(2)}) async-start(s8[16809984]{0:T(1024)(128)(4,1)} %bitcast.969), calls=%async_computation.54 | async-start | bytes 65536
  185.7 312.2 %collective-permute-start.8 = (bf16[2,2,2,152]{3,2,1,0:T(2,128)(2,1)S(1)}, bf16[2,2,2,152]{3,2,1,0:T(2,128)(2,1)S(1)}, u32[]{:S(2)}, u32[]{:S(2)}) collective-permute-start(bf16[2,2,2,152]{3,2,1,0:T(2,128)(2,1)S(1)} %broadcast_select_fusion), channel_id=1, source_target_pairs={{4,0},{6,2},{8,4},{10,6},{12,8},{14,10},{16,12},{18,14},{20,16},{2... | collective-permute-start | bytes 7304 | tf_op jit(solution)/shard_map/ppermute | solution.py:33
  189.9 309.9 %collective-permute-start.7 = (bf16[2,2,2,152]{3,2,1,0:T(2,128)(2,1)S(1)}, bf16[2,2,2,152]{3,2,1,0:T(2,128)(2,1)S(1)}, u32[]{:S(2)}, u32[]{:S(2)}) collective-permute-start(bf16[2,2,2,152]{3,2,1,0:T(2,128)(2,1)S(1)} %broadcast_select_fusion), channel_id=1, source_target_pairs={{0,4},{2,6},{4,8},{6,10},{8,12},{10,14},{12,16},{14,18},{16,20},{1... | collective-permute-start | bytes 7304 | tf_op jit(solution)/shard_map/ppermute | solution.py:33
  477.7 18.3 %copy-start.7 = (u32[128]{0:T(128)S(1)}, u32[128]{0:T(128)}, u32[]{:S(2)}) copy-start(u32[128]{0:T(128)} %constant.47) | copy-start | bytes 1540
  477.7 20.2 %copy-start.4 = (bf16[2,8,8,152]{3,2,1,0:T(8,128)(2,1)S(1)}, bf16[2,8,8,152]{3,2,1,0:T(8,128)(2,1)}, u32[]{:S(2)}) copy-start(bf16[2,8,8,152]{3,2,1,0:T(8,128)(2,1)} %get-tuple-element.19) | copy-start | bytes 116740
  497.9 44.0 %collective-permute-start.2 = (bf16[2,8,8,152]{3,2,1,0:T(8,128)(2,1)S(1)}, bf16[2,8,8,152]{3,2,1,0:T(8,128)(2,1)S(1)}, u32[]{:S(2)}, u32[]{:S(2)}) collective-permute-start(bf16[2,8,8,152]{3,2,1,0:T(8,128)(2,1)S(1)} %copy-done.4), channel_id=1, source_target_pairs={{0,2},{2,4},{4,6},{6,8},{8,10},{10,12},{12,14},{14,16},{16,18},{18... | collective-permute-start | bytes 116744 | tf_op jit(solution)/shard_map/ppermute | solution.py:14
  499.8 71.5 %collective-permute-start.1 = (bf16[2,16,16,152]{3,2,1,0:T(8,128)(2,1)}, bf16[2,16,16,152]{3,2,1,0:T(8,128)(2,1)S(1)}, u32[]{:S(2)}, u32[]{:S(2)}) collective-permute-start(bf16[2,16,16,152]{3,2,1,0:T(8,128)(2,1)} %get-tuple-element.16), channel_id=1, source_target_pairs={{2,0},{4,2},{6,4},{8,6},{10,8},{12,10},{14,12},{16,14},{18,16},{20... | collective-permute-start | bytes 466952 | tf_op jit(solution)/shard_map/ppermute | solution.py:15
  528.6 42.8 %collective-permute-start = (bf16[2,16,16,152]{3,2,1,0:T(8,128)(2,1)}, bf16[2,16,16,152]{3,2,1,0:T(8,128)(2,1)S(1)}, u32[]{:S(2)}, u32[]{:S(2)}) collective-permute-start(bf16[2,16,16,152]{3,2,1,0:T(8,128)(2,1)} %get-tuple-element.15), channel_id=1, source_target_pairs={{0,2},{2,4},{4,6},{6,8},{8,10},{10,12},{12,14},{14,16},{16,18},{18... | collective-permute-start | bytes 466952 | tf_op jit(solution)/shard_map/ppermute | solution.py:14
  571.3 135.3 %reduce-scatter.8.cloned.1.call-start = ((), (), s32[]{:S(2)}) async-start(), calls=%async_computation.1 | async-start | bytes 1867776
  (52 other events, 360.6 us)
Sparse Core Ops, SparseCore 0:
  571.4 25.5 all-reduce.9
  686.0 13.1 reduce-scatter.7
where the time goes:
time: 726 us; the launch traced here: 717 us
  local copies, waits for them, and re-layouts  539 us (74%)
  matrix products  92.3 us (13%)
  starting transfers between devices  39 us (5%)
  other arithmetic  26.2 us (4%)
  between operations  16.8 us (2%)
    unnamed x248, local copies, waits for them, and re-layouts  219 us
    reshape x8, local copies, waits for them, and re-layouts, parity_kernels(): kernels.append(window.reshape(-1, channels))  146 us
    dot_general x32, matrix products, far_field(): jnp.dot(stacked, kernel, preferred_element_type=jnp.float32)  89.4 us
    slice x1, local copies, waits for them, and re-layouts, parity_kernels(): masked_ops[1 - parity_x:7 - parity_x, 1 - parity_y:7 - parity_y, 1 - pari...  86 us
    dynamic_slice x4, local copies, waits for them, and re-layouts, parity_kernels(): window = lax.dynamic_slice_in_dim(window, source_parity, 1, 3)  44.7 us
    ppermute x3, starting transfers between devices, with_halo(): after = lax.ppermute(initial, axis, down)  25.5 us
    reshape x3, local copies, waits for them, and re-layouts, far_field(): jnp.stack(sections, axis=3).reshape(count_x * count_y * count_z, -1)  21.6 us
    mul x1, other arithmetic, shards(): masked_ops = translation_ops * near_blocks(translation_ops.dtype)  18.6 us
  transfers between devices with their start and end apart: 11, of which 1 were waited for; matrix products, arithmetic and copies ran while one was open for 90% of the time, Pallas kernels for 0%

commit v1 on v0

v1 whole, which is shorter than its diff:
```python
import jax
import jax.numpy as jnp
from jax import lax
from jax.experimental import pallas as pl
from jax.experimental.pallas import tpu as pltpu
from jax.sharding import PartitionSpec as P

BF = jnp.bfloat16
F32 = jnp.float32
MESH = pl.DeviceIdType.MESH
CH = 152
MAIN = 128
TAIL = CH - MAIN
ROWS = 160
NBLK = 10


def pad_tail(x):
    zeros = jnp.zeros(x.shape[:-1] + (MAIN - TAIL,), x.dtype)
    return jnp.concatenate([x, zeros], axis=x.ndim - 1)


def kernel(
    mf, mm, mc, mt, tr, up, out,
    tm, tt, um, ut, gb0, gb1, gb2, gb3,
    f0, t0, f1, t1, f2, t2, f3, t3,
    xb, xs, v, vu, acc, pm, pt, om, ot,
    tsem, gsem, send, recv,
):
    col = lax.axis_index("space")
    lev = lax.axis_index("level")
    n_col = lax.axis_size("space")
    par = col // 2
    base = 2 * par
    odd = lax.rem(col, 2)
    lo_ok = par > 0
    hi_ok = par < n_col // 2 - 1

    barrier = pltpu.get_barrier_semaphore()

    def greet(dev):
        pl.semaphore_signal(barrier, inc=1, device_id=(dev, lev), device_id_type=MESH)

    greet(base + 1 - odd)

    @pl.when(lo_ok)
    def _():
        greet(base - 2)
        greet(base - 1)

    @pl.when(hi_ok)
    def _():
        greet(base + 2)
        greet(base + 3)

    y0 = 6 * lev
    d0 = 2 * (1 - lev)
    y1 = 2 * lev
    loc0 = pltpu.make_async_copy(mf.at[:, pl.ds(y0, 10)], gb0.at[2:10, pl.ds(d0, 10)], gsem.at[0])
    loc1 = pltpu.make_async_copy(mm.at[:, pl.ds(y1, 6)], gb1.at[2:6, pl.ds(d0, 6)], gsem.at[1])
    loc2 = pltpu.make_async_copy(mc, gb2.at[2:4, pl.ds(d0, 4)], gsem.at[2])
    loc3 = pltpu.make_async_copy(mt, gb3.at[pl.ds(2 + odd, 1)], gsem.at[3])
    loc0.start()
    loc1.start()
    loc2.start()
    loc3.start()

    tcopies = {}

    def tcopy(kx, ysl, zsl, i):
        a = pltpu.make_async_copy(
            tr.at[kx, ysl, zsl, :, 0:MAIN], tm.at[kx, ysl, zsl, 0:CH, :], tsem.at[2 * i]
        )
        b = pltpu.make_async_copy(
            tr.at[kx, ysl, zsl, :, MAIN:CH], tt.at[kx, ysl, zsl, 0:CH, :], tsem.at[2 * i + 1]
        )
        a.start()
        b.start()
        tcopies.setdefault(kx, []).extend([a, b])

    idx = 0
    for kx in (2, 3, 4, 1, 0, 5, 6):
        if 2 <= kx <= 4:
            pieces = [
                (slice(0, 2), slice(0, 7)),
                (slice(5, 7), slice(0, 7)),
                (slice(2, 5), slice(0, 2)),
                (slice(2, 5), slice(5, 7)),
            ]
        else:
            pieces = [(slice(0, 7), slice(0, 7))]
        for ysl, zsl in pieces:
            tcopy(kx, ysl, zsl, idx)
            idx += 1
    cu_m = pltpu.make_async_copy(up.at[:, :, :, :, 0:MAIN], um.at[:, :, :, 0:CH, :], gsem.at[4])
    cu_t = pltpu.make_async_copy(up.at[:, :, :, :, MAIN:CH], ut.at[:, :, :, 0:CH, :], gsem.at[5])
    cu_m.start()
    cu_t.start()

    def halo(src, dst, i, dev, j=None):
        return pltpu.make_async_remote_copy(
            src_ref=src, dst_ref=dst, send_sem=send.at[i], recv_sem=recv.at[i if j is None else j],
            device_id=(dev, lev), device_id_type=MESH,
        )

    rights = [
        halo(mf.at[6:8, pl.ds(y0, 10)], gb0.at[0:2, pl.ds(d0, 10)], 0, col + 1),
        halo(mm.at[2:4, pl.ds(y1, 6)], gb1.at[0:2, pl.ds(d0, 6)], 1, col + 1),
        halo(mc, gb2.at[0:2, pl.ds(d0, 4)], 2, col + 1),
    ]
    lefts = [
        halo(mf.at[0:2, pl.ds(y0, 10)], gb0.at[10:12, pl.ds(d0, 10)], 3, col - 1),
        halo(mm.at[0:2, pl.ds(y1, 6)], gb1.at[6:8, pl.ds(d0, 6)], 4, col - 1),
        halo(mc, gb2.at[4:6, pl.ds(d0, 4)], 5, col - 1),
    ]
    top_partner = halo(mt, gb3.at[pl.ds(2 + odd, 1)], 6, base + 1 - odd)
    top_low = [
        halo(mt, gb3.at[pl.ds(4 + odd, 1)], 7 + i, base - 2 + i, 7 + odd) for i in range(2)
    ]
    top_high = [halo(mt, gb3.at[pl.ds(odd, 1)], 9 + i, base + 2 + i, 9 + odd) for i in range(2)]
    n_greet = 1 + jnp.where(lo_ok, 2, 0) + jnp.where(hi_ok, 2, 0)
    pl.semaphore_wait(barrier, n_greet)

    top_partner.start()

    @pl.when(lo_ok)
    def _():
        for c in top_low:
            c.start()

    @pl.when(hi_ok)
    def _():
        for c in top_high:
            c.start()

    @pl.when(col < n_col - 1)
    def _():
        for c in rights[::-1]:
            c.start()

    @pl.when(col > 0)
    def _():
        for c in lefts[::-1]:
            c.start()

    gb0[:, pl.ds(10 * lev, 2)] = jnp.zeros((12, 2, 16, CH), BF)
    gb1[:, pl.ds(6 * lev, 2)] = jnp.zeros((8, 2, 8, CH), BF)
    gb2[:, pl.ds(4 * lev, 2)] = jnp.zeros((6, 2, 4, CH), BF)

    @pl.when(col == 0)
    def _():
        gb0[0:2] = jnp.zeros((2, 12, 16, CH), BF)
        gb1[0:2] = jnp.zeros((2, 8, 8, CH), BF)
        gb2[0:2] = jnp.zeros((2, 6, 4, CH), BF)

    @pl.when(col == n_col - 1)
    def _():
        gb0[10:12] = jnp.zeros((2, 12, 16, CH), BF)
        gb1[6:8] = jnp.zeros((2, 8, 8, CH), BF)
        gb2[4:6] = jnp.zeros((2, 6, 4, CH), BF)

    @pl.when(par == 0)
    def _():
        gb3[0:2] = jnp.zeros((2, 2, 2, CH), BF)

    @pl.when(par == n_col // 2 - 1)
    def _():
        gb3[4:6] = jnp.zeros((2, 2, 2, CH), BF)

    def zero_edges(i, _):
        tm[i // 7, lax.rem(i, 7), :, CH:ROWS, :] = jnp.zeros((7, ROWS - CH, MAIN), BF)
        tt[i // 7, lax.rem(i, 7), :, CH:ROWS, :] = jnp.zeros((7, ROWS - CH, TAIL), BF)
        return 0

    lax.fori_loop(0, 49, zero_edges, 0)

    def zero_near(i, _):
        kx, ky, kz = 2 + i // 9, 2 + lax.rem(i // 3, 3), 2 + lax.rem(i, 3)
        tm[kx, ky, kz, 0:CH, :] = jnp.zeros((CH, MAIN), BF)
        tt[kx, ky, kz, 0:CH, :] = jnp.zeros((CH, TAIL), BF)
        return 0

    lax.fori_loop(0, 27, zero_near, 0)
    um[:, :, :, CH:ROWS, :] = jnp.zeros((2, 2, 2, ROWS - CH, MAIN), BF)
    ut[:, :, :, CH:ROWS, :] = jnp.zeros((2, 2, 2, ROWS - CH, TAIL), BF)
    f3[...] = jnp.zeros(f3.shape, F32)
    t3[...] = jnp.zeros(t3.shape, F32)

    def z_slots(tail, sy):
        even = lax.rem(lax.broadcasted_iota(jnp.int32, tail.shape, 0), 2) == 0
        a = pltpu.roll(tail, 64 * sy, 1) if sy else tail
        b = pltpu.roll(tail, 64 * sy + 32, 1)
        return jnp.where(even, a, b)

    z8 = jnp.zeros((8, MAIN), F32)

    def conv0(i, _):
        x, yp = i // 6, lax.rem(i, 6)
        tails = []
        for sy in range(2):
            y = 2 * yp + sy
            f0[x, y, 0:8, :] = z8
            f0[x, y, 24:32, :] = z8
            f0[x, y, 8:24, :] = gb0[x, y, :, 0:MAIN].astype(F32)
            tails.append(z_slots(pad_tail(gb0[x, y, :, MAIN:CH].astype(F32)), sy))
        t0[x, yp, 0:8, :] = z8
        t0[x, yp, 24:32, :] = z8
        t0[x, yp, 8:24, :] = tails[0] + tails[1]
        return 0

    def build0(i, _):
        xp, w = i // 9, lax.rem(i, 9)
        sty, stz = w // 3, lax.rem(w, 3)
        for sx in range(2):
            x = 2 * xp + sx
            for sy in range(2):
                for sz in range(2):
                    rows = [
                        f0[x, 2 * (py + sty) + sy, pl.ds(6 + 2 * stz + sz, 8, stride=2), :]
                        for py in range(4)
                    ]
                    s = 4 * sx + 2 * sy + sz
                    xb[w, s, xp] = jnp.concatenate(rows, axis=0).astype(BF)
            rows = [
                t0[x, py + sty, pl.ds(6 + 2 * stz, 8, stride=2), :]
                + t0[x, py + sty, pl.ds(7 + 2 * stz, 8, stride=2), :]
                for py in range(4)
            ]
            xb[w, 8 + sx, xp] = jnp.concatenate(rows, axis=0).astype(BF)
        return 0

    loc0.wait()
    lax.fori_loop(12, 60, conv0, 0)
    lax.fori_loop(9, 45, build0, 0)

    loc1.wait()
    loc2.wait()
    loc3.wait()

    @pl.when(col > 0)
    def _():
        for c in rights:
            c.wait_recv()

    @pl.when(col < n_col - 1)
    def _():
        for c in lefts:
            c.wait_recv()

    halo(mt, gb3.at[pl.ds(3 - odd, 1)], 6, base + 1 - odd).wait_recv()

    @pl.when(lo_ok)
    def _():
        for i in range(2):
            halo(mt, gb3.at[pl.ds(i, 1)], 9 + i, base - 2 + i).wait_recv()

    @pl.when(hi_ok)
    def _():
        for i in range(2):
            halo(mt, gb3.at[pl.ds(4 + i, 1)], 7 + i, base + 2 + i).wait_recv()

    lax.fori_loop(0, 12, conv0, 0)
    lax.fori_loop(60, 72, conv0, 0)
    lax.fori_loop(0, 9, build0, 0)
    lax.fori_loop(45, 54, build0, 0)

    def conv1(x, _):
        for sy in range(2):
            f1[x, sy, 0:8, :] = z8
            f1[x, sy, 40:48, :] = z8
        t1[x, 0:8, :] = z8
        t1[x, 40:48, :] = z8
        for yp in range(4):
            tails = []
            for sy in range(2):
                y = 2 * yp + sy
                f1[x, sy, 8 + 8 * yp : 16 + 8 * yp, :] = gb1[x, y, :, 0:MAIN].astype(F32)
                tails.append(z_slots(pad_tail(gb1[x, y, :, MAIN:CH].astype(F32)), sy))
            t1[x, 8 + 8 * yp : 16 + 8 * yp, :] = tails[0] + tails[1]
        return 0

    lax.fori_loop(0, 8, conv1, 0)

    def conv2(i, _):
        x, yp = i // 3, lax.rem(i, 3)
        tails = []
        for sy in range(2):
            y = 2 * yp + sy
            f2[x, y] = jnp.zeros((32, MAIN), F32)
            f2[x, y, 8:12, :] = gb2[x, y, :, 0:MAIN].astype(F32)
            tails.append(z_slots(pad_tail(gb2[x, y, :, MAIN:CH].astype(F32)), sy))
        t2[x, yp] = jnp.zeros((32, MAIN), F32)
        t2[x, yp, 8:12, :] = tails[0] + tails[1]
        return 0

    lax.fori_loop(0, 18, conv2, 0)

    def conv3(x, _):
        tails = []
        for y in range(2):
            f3[x, 2 + y, 8:10, :] = gb3[x, y, :, 0:MAIN].astype(F32)
            tails.append(z_slots(pad_tail(gb3[x, y, :, MAIN:CH].astype(F32)), y))
        t3[x, 1, 8:10, :] = tails[0] + tails[1]
        return 0

    lax.fori_loop(0, 6, conv3, 0)

    def build_small(i, _):
        stx, sty, stz = i // 9, lax.rem(i // 3, 3), lax.rem(i, 3)
        row = lax.broadcasted_iota(jnp.int32, (8, MAIN), 0)
        pz = lax.rem(row, 4) + stz - 1
        inside = (pz >= 0) & (pz < 4)

        def put(j, one, two, three):
            one = [jnp.where(inside, p, 0.0) for p in one]
            rest = jnp.where(row < 2, two, jnp.where(row == 2, three, 0.0))
            xs[i, j] = jnp.concatenate(one + [rest, z8], axis=0).astype(BF)

        for sx in range(2):
            for sy in range(2):
                for sz in range(2):
                    one = [
                        f1[2 * (px + stx) + sx, sy, pl.ds(6 + 8 * sty + 2 * stz + sz, 8, stride=2), :]
                        for px in range(2)
                    ]
                    two = f2[2 * stx + sx, 2 * sty + sy, pl.ds(6 + 2 * stz + sz, 8, stride=2), :]
                    three = f3[2 * stx + sx, 2 * sty + sy, pl.ds(2 + 2 * stz + sz, 8, stride=2), :]
                    put(4 * sx + 2 * sy + sz, one, two, three)
            one = [
                t1[2 * (px + stx) + sx, pl.ds(6 + 8 * sty + 2 * stz, 8, stride=2), :]
                + t1[2 * (px + stx) + sx, pl.ds(7 + 8 * sty + 2 * stz, 8, stride=2), :]
                for px in range(2)
            ]
            two = (
                t2[2 * stx + sx, sty, pl.ds(6 + 2 * stz, 8, stride=2), :]
                + t2[2 * stx + sx, sty, pl.ds(7 + 2 * stz, 8, stride=2), :]
            )
            three = (
                t3[2 * stx + sx, sty, pl.ds(2 + 2 * stz, 8, stride=2), :]
                + t3[2 * stx + sx, sty, pl.ds(3 + 2 * stz, 8, stride=2), :]
            )
            put(8 + sx, one, two, three)
        return 0

    lax.fori_loop(0, 27, build_small, 0)

    def tails_of(kx):
        def body(rz, _):
            last = None
            for ky in range(7):
                a = pad_tail(tt[kx, ky, rz + 1])
                b = pad_tail(tt[kx, ky, rz])
                pair = a + pltpu.roll(b, 32, 1)
                if last is not None:
                    v[(kx * 6 + ky - 1) * 6 + rz] = pair + last
                last = pltpu.roll(pair, 64, 1)
            return 0

        lax.fori_loop(0, 6, body, 0)

    def step(i, stx):
        sty, stz = i // 3, lax.rem(i, 3)
        t = stx * 9 + i
        lhs = jnp.concatenate(
            [
                jnp.concatenate(
                    [xb[i, j, stx : stx + 4].reshape(128, MAIN), xs[t, j]], axis=0
                )
                for j in range(NBLK)
            ],
            axis=1,
        )

        def accumulate(n, pick):
            mains = []
            tails = []
            for s in range(8):
                w = pick(s)
                mains.append(jnp.concatenate([x(0, MAIN) for x in w], axis=1))
                tails.append(jnp.concatenate([x(MAIN, ROWS) for x in w], axis=1))
            rhs = jnp.concatenate(mains + tails, axis=0)
            res = jnp.dot(lhs, rhs, preferred_element_type=F32)
            acc[2 * n] += res[:, 0:MAIN]
            acc[2 * n + 1] += res[:, MAIN:]

        def main_of(s, c):
            kx = 2 * stx + (s >> 2) - (c >> 2) + 1
            ky = 2 * sty + ((s >> 1) & 1) - ((c >> 1) & 1) + 1
            kz = 2 * stz + (s & 1) - (c & 1) + 1
            return lambda lo, hi: tm[kx, ky, kz, lo:hi, :]

        def tail_of(s, h):
            kx = 2 * stx + (s >> 2) - h + 1
            ry = 2 * sty + ((s >> 1) & 1)
            rz = 2 * stz + (s & 1)
            k = (kx * 6 + ry) * 6 + rz
            return lambda lo, hi: v[k, lo:hi, :]

        for n in range(4):
            accumulate(n, lambda s: [main_of(s, 2 * n), main_of(s, 2 * n + 1)])
        accumulate(4, lambda s: [tail_of(s, 0), tail_of(s, 1)])

    acc[...] = jnp.zeros(acc.shape, F32)
    for stx, slabs in ((1, (2, 3, 4)), (0, (1, 0)), (2, (5, 6))):
        for kx in slabs:
            for c in tcopies[kx]:
                c.wait()
            tails_of(kx)
        if stx == 1:

            def body(i, _):
                step(i + jnp.where(i >= 4, 1, 0), 1)
                return 0

            lax.fori_loop(0, 8, body, 0)
        else:

            def body(i, _, stx=stx):
                step(i, stx)
                return 0

            lax.fori_loop(0, 9, body, 0)

    cu_m.wait()
    cu_t.wait()
    for h in range(2):
        parts = [pad_tail(ut[h, q >> 1, q & 1]) for q in range(4)]
        total = parts[0]
        for q in range(1, 4):
            total = total + pltpu.roll(parts[q], 32 * q, 1)
        vu[h] = total

    def upsampled(main, tail):
        rows = main.shape[0]
        hi_m = main.astype(BF)
        lo_m = (main - hi_m.astype(F32)).astype(BF)
        hi_t = tail.astype(BF).astype(F32)
        both = (hi_t + pltpu.roll(tail - hi_t, 32, 1)).astype(BF)
        lhs = jnp.concatenate([hi_m, lo_m, both], axis=1)

        def rhs_of(x):
            return jnp.concatenate(
                [x(0, MAIN), x(0, MAIN), x(MAIN, ROWS), x(MAIN, ROWS), jnp.zeros((64, MAIN), BF)],
                axis=0,
            )

        cols = []
        for n in range(5):
            if n < 4:
                pair = [
                    rhs_of(lambda lo, hi, c=c: um[c >> 2, (c >> 1) & 1, c & 1, lo:hi, :])
                    for c in (2 * n, 2 * n + 1)
                ]
            else:
                pair = [rhs_of(lambda lo, hi, h=h: vu[h, lo:hi, :]) for h in range(2)]
            res = jnp.dot(lhs, jnp.concatenate(pair, axis=1), preferred_element_type=F32)
            cols += [res[:, 0:MAIN], res[:, MAIN:]]
        return cols

    def tail_lanes(x, c):
        q = c & 3
        y = pltpu.roll(x, MAIN - 32 * q, 1) if q else x
        lane = lax.broadcasted_iota(jnp.int32, x.shape, 1)
        return jnp.where(lane < TAIL, y, 0.0)

    pm[...] = jnp.zeros(pm.shape, F32)
    pt[...] = jnp.zeros(pt.shape, F32)
    rest = [acc[j, 144:152, :] for j in range(NBLK)]
    for cz in range(2):
        mains = [rest[4 * a + 2 * b + cz] for a in range(2) for b in range(2)]
        tails = [
            tail_lanes(rest[8 + a], 4 * a + 2 * b + cz) for a in range(2) for b in range(2)
        ]

        def choose(four):
            low = jnp.where(lev == 0, four[0], four[1])
            high = jnp.where(lev == 0, four[2], four[3])
            return jnp.where(odd == 0, low, high)

        pm[cz : cz + 1, :] = choose(mains)[2:3]
        pt[cz : cz + 1, :] = choose(tails)[2:3]
    add = upsampled(pm[0:16, :], pt[0:16, :])
    local2 = [rest[j] + add[j][0:8] for j in range(NBLK)]
    for c in range(8):
        cx, cy, cz = c >> 2, (c >> 1) & 1, c & 1
        tail = tail_lanes(local2[8 + cx], c)
        for p in range(2):
            r = 8 * cx + 4 * cy + 2 * p + cz
            pm[16 + r : 17 + r, :] = local2[c][p : p + 1]
            pt[16 + r : 17 + r, :] = tail[p : p + 1]
    add = upsampled(pm[16:32, :], pt[16:32, :])
    local1 = [acc[j, 128:144, :] + add[j] for j in range(NBLK)]
    for c in range(8):
        cx, cy, cz = c >> 2, (c >> 1) & 1, c & 1
        tail = tail_lanes(local1[8 + cx], c)
        for px in range(2):
            for py in range(2):
                r = 32 + 32 * (2 * px + cx) + 8 * (2 * py + cy) + cz
                q = 8 * px + 4 * py
                pm[pl.ds(r, 4, stride=2), :] = local1[c][q : q + 4]
                pt[pl.ds(r, 4, stride=2), :] = tail[q : q + 4]
    add = upsampled(pm[32:160, :], pt[32:160, :])
    for c in range(8):
        cx, cy, cz = c >> 2, (c >> 1) & 1, c & 1
        main = acc[c, 0:128, :] + add[c]
        tail = tail_lanes(acc[8 + cx, 0:128, :] + add[8 + cx], c)
        for px in range(4):
            for py in range(4):
                q = 32 * px + 8 * py
                x, y = 2 * px + cx, 2 * py + cy
                om[8 * x + y, pl.ds(cz, 8, stride=2), :] = main[q : q + 8]
                ot[8 * x + y, pl.ds(cz, 8, stride=2), :] = tail[q : q + 8]

    def emit(x, _):
        for y in range(8):
            out[x, y, :, 0:MAIN] = om[8 * x + y]
            out[x, y, :, MAIN:CH] = ot[8 * x + y][:, 0:TAIL]
        return 0

    lax.fori_loop(0, 8, emit, 0)

    top_partner.wait_send()

    @pl.when(lo_ok)
    def _():
        for c in top_low:
            c.wait_send()

    @pl.when(hi_ok)
    def _():
        for c in top_high:
            c.wait_send()

    @pl.when(col < n_col - 1)
    def _():
        for c in rights:
            c.wait_send()

    @pl.when(col > 0)
    def _():
        for c in lefts:
            c.wait_send()


def shards(
    multipole_fine, multipole_mid, multipole_coarse, multipole_top, translation_ops, upsample_ops
):
    vmem = pltpu.VMEM
    return pl.pallas_call(
        kernel,
        out_shape=jax.ShapeDtypeStruct((8, 8, 16, CH), F32),
        in_specs=[pl.BlockSpec(memory_space=pl.ANY)] * 6,
        out_specs=pl.BlockSpec(memory_space=pltpu.VMEM),
        scratch_shapes=[
            vmem((7, 7, 7, ROWS, MAIN), BF),
            vmem((7, 7, 7, ROWS, TAIL), BF),
            vmem((2, 2, 2, ROWS, MAIN), BF),
            vmem((2, 2, 2, ROWS, TAIL), BF),
            vmem((12, 12, 16, CH), BF),
            vmem((8, 8, 8, CH), BF),
            vmem((6, 6, 4, CH), BF),
            vmem((6, 2, 2, CH), BF),
            vmem((12, 12, 32, MAIN), F32),
            vmem((12, 6, 32, MAIN), F32),
            vmem((8, 2, 48, MAIN), F32),
            vmem((8, 48, MAIN), F32),
            vmem((6, 6, 32, MAIN), F32),
            vmem((6, 3, 32, MAIN), F32),
            vmem((6, 6, 32, MAIN), F32),
            vmem((6, 3, 32, MAIN), F32),
            vmem((9, NBLK, 6, 32, MAIN), BF),
            vmem((27, NBLK, 32, MAIN), BF),
            vmem((7 * 36, ROWS, MAIN), BF),
            vmem((2, ROWS, MAIN), BF),
            vmem((NBLK, 160, MAIN), F32),
            vmem((160, MAIN), F32),
            vmem((160, MAIN), F32),
            vmem((64, 16, MAIN), F32),
            vmem((64, 16, MAIN), F32),
            pltpu.SemaphoreType.DMA((32,)),
            pltpu.SemaphoreType.DMA((6,)),
            pltpu.SemaphoreType.DMA((11,)),
            pltpu.SemaphoreType.DMA((11,)),
        ],
        compiler_params=pltpu.CompilerParams(
            collective_id=0, has_side_effects=True, vmem_limit_bytes=66_000_000
        ),
        name="downward",
    )(multipole_fine, multipole_mid, multipole_coarse, multipole_top, translation_ops, upsample_ops)


def solution(mesh):
    placed = (
        P("space", None, None, None),
        P("space", None, None, None),
        P("space", None, None, None),
        P("space", None, None, None),
        P(),
        P(),
    )
    return jax.shard_map(
        shards,
        mesh=mesh,
        in_specs=placed,
        out_specs=P("space", "level", None, None),
        check_vma=False,
    )
```

time: 726 us -> 54.9 us (0.08); the launches traced: 717 us -> 54.7 us
  local copies, waits for them, and re-layouts: 539 us -> 2.26 us
  matrix products: 92.3 us -> 0 us
  Pallas kernels: 0 us -> 52.5 us
  starting transfers between devices: 39 us -> 0 us
  other arithmetic: 26.2 us -> 0 us
  between operations: 16.8 us -> 0.01 us
    unnamed x248 -> x1, local copies, waits for them, and re-layouts: 219 us -> 2.26 us
    reshape x21 -> x0, local copies, waits for them, and re-layouts: 177 us -> none  [the longest x8 146 us: parity_kernels(): kernels.append(window.reshape(-1, channels))]
    dot_general x35 -> x0, matrix products: 92.3 us -> none  [the longest x32 89.4 us: far_field(): jnp.dot(stacked, kernel, preferred_element_type=jnp.float32)]
    slice x3 -> x0, local copies, waits for them, and re-layouts: 88.4 us -> none  [the longest x1 86 us: parity_kernels(): masked_ops[1 - parity_x:7 - parity_x, 1 - parity_y:7 - parity_y, 1 - pari...]
    pallas_call x0 -> x1, Pallas kernels: none -> 52.5 us  [shards(): pl.pallas_call(kernel, out_shape=jax.ShapeDtypeStruct((8, 8, 16, CH), F32...]
    dynamic_slice x8 -> x0, local copies, waits for them, and re-layouts: 47 us -> none  [the longest x4 44.7 us: parity_kernels(): window = lax.dynamic_slice_in_dim(window, source_parity, 1, 3)]
    ppermute x9 -> x0, starting transfers between devices: 39 us -> none  [the longest x3 25.5 us: with_halo(): after = lax.ppermute(initial, axis, down)]
    mul x1 -> x0, other arithmetic: 18.6 us -> none  [shards(): masked_ops = translation_ops * near_blocks(translation_ops.dtype)]
  transfers between devices with their start and end apart: 11 -> 0, of which waited for: 1 -> 0; matrix products, arithmetic and copies ran while one was open for 90% -> 0% of each run, Pallas kernels for 0% -> 0%
where the time goes in v1:
time: 54.9 us; the launch traced here: 54.7 us
  Pallas kernels  52.5 us (96%)
  local copies, waits for them, and re-layouts  2.26 us (4%)
    pallas_call x1, Pallas kernels, shards(): pl.pallas_call(kernel, out_shape=jax.ShapeDtypeStruct((8, 8, 16, CH), F32...  52.5 us
    unnamed x1, local copies, waits for them, and re-layouts  2.26 us

profile of v1, /device:TPU:6, one launch (start us, length us, event | category | flops | bytes accessed | tf_op | source)
XLA Modules:
  0.0 54.7 jit_solution(17267029008594338503)
XLA Ops:
  0.0 52.5 %downward.1 = f32[8,8,16,152]{3,2,1,0:T(8,128)} custom-call(bf16[8,16,16,152]{3,2,1,0:T(8,128)(2,1)} %mf.1, bf16[4,8,8,152]{3,2,1,0:T(8,128)(2,1)} %mm.1, bf16[2,4,4,152]{3,2,1,0:T(4,128)(2,1)} %mc.1, bf16[1,2,2,152]{3,2,1,0:T(2,128)(2,1)} %mt.1, bf16[7,7,7,152,152]{4,3,2,1,0:T(8,128)(2,1)} %tr.1, bf16[2,2,2,152,152]{4,3,2,1,0:T(8,128)(2,1)} %up.1), custom_call_target="tpu_custom_call" | custom-call | tf_op jit(solution)/shard_map/downward/pallas_call | solution.py:549
  52.5 2.3 %copy.8 = f32[8,8,16,152]{3,2,1,0:T(8,128)} copy(f32[8,8,16,152]{3,2,1,0:T(8,128)} %downward.1) | data formatting | bytes 1245184

commit v2 on v1

--- a/solution.py
+++ b/solution.py
@@ -24,7 +24,7 @@
     mf, mm, mc, mt, tr, up, out,
     tm, tt, um, ut, gb0, gb1, gb2, gb3,
     f0, t0, f1, t1, f2, t2, f3, t3,
-    xb, xs, v, vu, acc, pm, pt, om, ot,
+    xm, xe, xsm, xse, v, vu, acc, pm, pt, om, ot,
     tsem, gsem, send, recv,
 ):
     col = lax.axis_index("space")
@@ -119,30 +119,7 @@
     ]
     top_high = [halo(mt, gb3.at[pl.ds(odd, 1)], 9 + i, base + 2 + i, 9 + odd) for i in range(2)]
     n_greet = 1 + jnp.where(lo_ok, 2, 0) + jnp.where(hi_ok, 2, 0)
-    pl.semaphore_wait(barrier, n_greet)
-
-    top_partner.start()
-
-    @pl.when(lo_ok)
-    def _():
-        for c in top_low:
-            c.start()
-
-    @pl.when(hi_ok)
-    def _():
-        for c in top_high:
-            c.start()
-
-    @pl.when(col < n_col - 1)
-    def _():
-        for c in rights[::-1]:
-            c.start()
-
-    @pl.when(col > 0)
-    def _():
-        for c in lefts[::-1]:
-            c.start()
-
+    z8 = jnp.zeros((8, MAIN), F32)
     gb0[:, pl.ds(10 * lev, 2)] = jnp.zeros((12, 2, 16, CH), BF)
     gb1[:, pl.ds(6 * lev, 2)] = jnp.zeros((8, 2, 8, CH), BF)
     gb2[:, pl.ds(4 * lev, 2)] = jnp.zeros((6, 2, 4, CH), BF)
@@ -167,24 +144,53 @@
     def _():
         gb3[4:6] = jnp.zeros((2, 2, 2, CH), BF)
 
-    def zero_edges(i, _):
-        tm[i // 7, lax.rem(i, 7), :, CH:ROWS, :] = jnp.zeros((7, ROWS - CH, MAIN), BF)
-        tt[i // 7, lax.rem(i, 7), :, CH:ROWS, :] = jnp.zeros((7, ROWS - CH, TAIL), BF)
+    def zero_edges(kx, _):
+        for ky in range(7):
+            tm[kx, ky, :, CH:ROWS, :] = jnp.zeros((7, ROWS - CH, MAIN), BF)
+            tt[kx, ky, :, CH:ROWS, :] = jnp.zeros((7, ROWS - CH, TAIL), BF)
         return 0
 
-    lax.fori_loop(0, 49, zero_edges, 0)
+    lax.fori_loop(0, 7, zero_edges, 0)
 
     def zero_near(i, _):
-        kx, ky, kz = 2 + i // 9, 2 + lax.rem(i // 3, 3), 2 + lax.rem(i, 3)
-        tm[kx, ky, kz, 0:CH, :] = jnp.zeros((CH, MAIN), BF)
-        tt[kx, ky, kz, 0:CH, :] = jnp.zeros((CH, TAIL), BF)
+        for kz in range(2, 5):
+            tm[2 + i // 3, 2 + lax.rem(i, 3), kz, 0:CH, :] = jnp.zeros((CH, MAIN), BF)
+            tt[2 + i // 3, 2 + lax.rem(i, 3), kz, 0:CH, :] = jnp.zeros((CH, TAIL), BF)
         return 0
 
-    lax.fori_loop(0, 27, zero_near, 0)
+    lax.fori_loop(0, 9, zero_near, 0)
     um[:, :, :, CH:ROWS, :] = jnp.zeros((2, 2, 2, ROWS - CH, MAIN), BF)
     ut[:, :, :, CH:ROWS, :] = jnp.zeros((2, 2, 2, ROWS - CH, TAIL), BF)
-    f3[...] = jnp.zeros(f3.shape, F32)
-    t3[...] = jnp.zeros(t3.shape, F32)
+
+    def zero_pads(x, _):
+        for y in range(12):
+            f0[x, y, 0:8, :] = z8
+            f0[x, y, 24:32, :] = z8
+        for yp in range(6):
+            t0[x, yp, 0:8, :] = z8
+            t0[x, yp, 24:32, :] = z8
+        return 0
+
+    lax.fori_loop(0, 12, zero_pads, 0)
+
+    def zero_coarse(x, _):
+        f2[x] = jnp.zeros((6, 32, MAIN), F32)
+        f3[x] = jnp.zeros((6, 32, MAIN), F32)
+        t2[x] = jnp.zeros((3, 32, MAIN), F32)
+        t3[x] = jnp.zeros((3, 32, MAIN), F32)
+        return 0
+
+    lax.fori_loop(0, 6, zero_coarse, 0)
+
+    def zero_mid(x, _):
+        for sy in range(2):
+            f1[x, sy, 0:8, :] = z8
+            f1[x, sy, 40:48, :] = z8
+        t1[x, 0:8, :] = z8
+        t1[x, 40:48, :] = z8
+        return 0
+
+    lax.fori_loop(0, 8, zero_mid, 0)
 
     def z_slots(tail, sy):
         even = lax.rem(lax.broadcasted_iota(jnp.int32, tail.shape, 0), 2) == 0
@@ -192,25 +198,17 @@
         b = pltpu.roll(tail, 64 * sy + 32, 1)
         return jnp.where(even, a, b)
 
-    z8 = jnp.zeros((8, MAIN), F32)
-
-    def conv0(i, _):
-        x, yp = i // 6, lax.rem(i, 6)
-        tails = []
-        for sy in range(2):
-            y = 2 * yp + sy
-            f0[x, y, 0:8, :] = z8
-            f0[x, y, 24:32, :] = z8
-            f0[x, y, 8:24, :] = gb0[x, y, :, 0:MAIN].astype(F32)
-            tails.append(z_slots(pad_tail(gb0[x, y, :, MAIN:CH].astype(F32)), sy))
-        t0[x, yp, 0:8, :] = z8
-        t0[x, yp, 24:32, :] = z8
-        t0[x, yp, 8:24, :] = tails[0] + tails[1]
-        return 0
-
-    def build0(i, _):
-        xp, w = i // 9, lax.rem(i, 9)
-        sty, stz = w // 3, lax.rem(w, 3)
+    def conv0(x):
+        for yp in range(6):
+            tails = []
+            for sy in range(2):
+                y = 2 * yp + sy
+                f0[x, y, 8:24, :] = gb0[x, y, :, 0:MAIN].astype(F32)
+                tails.append(z_slots(pad_tail(gb0[x, y, :, MAIN:CH].astype(F32)), sy))
+            t0[x, yp, 8:24, :] = tails[0] + tails[1]
+
+    def build0(xp, w, store):
+        sty, stz = (w // 3, w % 3) if isinstance(w, int) else (w // 3, lax.rem(w, 3))
         for sx in range(2):
             x = 2 * xp + sx
             for sy in range(2):
@@ -219,94 +217,120 @@
                         f0[x, 2 * (py + sty) + sy, pl.ds(6 + 2 * stz + sz, 8, stride=2), :]
                         for py in range(4)
                     ]
-                    s = 4 * sx + 2 * sy + sz
-                    xb[w, s, xp] = jnp.concatenate(rows, axis=0).astype(BF)
+                    store(w, 4 * sx + 2 * sy + sz, jnp.concatenate(rows, axis=0).astype(BF))
             rows = [
                 t0[x, py + sty, pl.ds(6 + 2 * stz, 8, stride=2), :]
                 + t0[x, py + sty, pl.ds(7 + 2 * stz, 8, stride=2), :]
                 for py in range(4)
             ]
-            xb[w, 8 + sx, xp] = jnp.concatenate(rows, axis=0).astype(BF)
+            store(w, 8 + sx, jnp.concatenate(rows, axis=0).astype(BF))
+
+    with jax.named_scope("conv_own"):
+        loc0.wait()
+
+        def own_conv(x, _):
+            conv0(x)
+            return 0
+
+        lax.fori_loop(2, 10, own_conv, 0)
+
+    with jax.named_scope("greet"):
+        pl.semaphore_wait(barrier, n_greet)
+
+        top_partner.start()
+
+        @pl.when(lo_ok)
+        def _():
+            for c in top_low:
+                c.start()
+
+        @pl.when(hi_ok)
+        def _():
+            for c in top_high:
+                c.start()
+
+        @pl.when(col < n_col - 1)
+        def _():
+            for c in rights[::-1]:
+                c.start()
+
+        @pl.when(col > 0)
+        def _():
+            for c in lefts[::-1]:
+                c.start()
+
+    with jax.named_scope("build_own"):
+
+        def own_build(w, _):
+            for xp in range(1, 5):
+
+                def store(w, j, val, xp=xp):
+                    xm[w, j, xp - 1] = val
+
+                build0(xp, w, store)
+            return 0
+
+        lax.fori_loop(0, 9, own_build, 0)
+
+    with jax.named_scope("wait_small"):
+        loc1.wait()
+        loc2.wait()
+        loc3.wait()
+
+        @pl.when(col > 0)
+        def _():
+            for c in rights[1:]:
+                c.wait_recv()
+
+        @pl.when(col < n_col - 1)
+        def _():
+            for c in lefts[1:]:
+                c.wait_recv()
+
+        halo(mt, gb3.at[pl.ds(3 - odd, 1)], 6, base + 1 - odd).wait_recv()
+
+        @pl.when(lo_ok)
+        def _():
+            for i in range(2):
+                halo(mt, gb3.at[pl.ds(i, 1)], 9 + i, base - 2 + i).wait_recv()
+
+        @pl.when(hi_ok)
+        def _():
+            for i in range(2):
+                halo(mt, gb3.at[pl.ds(4 + i, 1)], 7 + i, base + 2 + i).wait_recv()
+
+    def conv1(i, _):
+        for k in range(2):
+            x = 2 * i + k
+            for yp in range(4):
+                tails = []
+                for sy in range(2):
+                    y = 2 * yp + sy
+                    f1[x, sy, 8 + 8 * yp : 16 + 8 * yp, :] = gb1[x, y, :, 0:MAIN].astype(F32)
+                    tails.append(z_slots(pad_tail(gb1[x, y, :, MAIN:CH].astype(F32)), sy))
+                t1[x, 8 + 8 * yp : 16 + 8 * yp, :] = tails[0] + tails[1]
         return 0
 
-    loc0.wait()
-    lax.fori_loop(12, 60, conv0, 0)
-    lax.fori_loop(9, 45, build0, 0)
-
-    loc1.wait()
-    loc2.wait()
-    loc3.wait()
-
-    @pl.when(col > 0)
-    def _():
-        for c in rights:
-            c.wait_recv()
-
-    @pl.when(col < n_col - 1)
-    def _():
-        for c in lefts:
-            c.wait_recv()
-
-    halo(mt, gb3.at[pl.ds(3 - odd, 1)], 6, base + 1 - odd).wait_recv()
-
-    @pl.when(lo_ok)
-    def _():
-        for i in range(2):
-            halo(mt, gb3.at[pl.ds(i, 1)], 9 + i, base - 2 + i).wait_recv()
-
-    @pl.when(hi_ok)
-    def _():
-        for i in range(2):
-            halo(mt, gb3.at[pl.ds(4 + i, 1)], 7 + i, base + 2 + i).wait_recv()
-
-    lax.fori_loop(0, 12, conv0, 0)
-    lax.fori_loop(60, 72, conv0, 0)
-    lax.fori_loop(0, 9, build0, 0)
-    lax.fori_loop(45, 54, build0, 0)
-
-    def conv1(x, _):
-        for sy in range(2):
-            f1[x, sy, 0:8, :] = z8
-            f1[x, sy, 40:48, :] = z8
-        t1[x, 0:8, :] = z8
-        t1[x, 40:48, :] = z8
-        for yp in range(4):
+    def conv23():
+        for x in range(6):
+            for yp in range(3):
+                tails = []
+                for sy in range(2):
+                    y = 2 * yp + sy
+                    f2[x, y, 8:12, :] = gb2[x, y, :, 0:MAIN].astype(F32)
+                    tails.append(z_slots(pad_tail(gb2[x, y, :, MAIN:CH].astype(F32)), sy))
+                t2[x, yp, 8:12, :] = tails[0] + tails[1]
             tails = []
-            for sy in range(2):
-                y = 2 * yp + sy
-                f1[x, sy, 8 + 8 * yp : 16 + 8 * yp, :] = gb1[x, y, :, 0:MAIN].astype(F32)
-                tails.append(z_slots(pad_tail(gb1[x, y, :, MAIN:CH].astype(F32)), sy))
-            t1[x, 8 + 8 * yp : 16 + 8 * yp, :] = tails[0] + tails[1]
-        return 0
-
-    lax.fori_loop(0, 8, conv1, 0)
-
-    def conv2(i, _):
-        x, yp = i // 3, lax.rem(i, 3)
-        tails = []
-        for sy in range(2):
-            y = 2 * yp + sy
-            f2[x, y] = jnp.zeros((32, MAIN), F32)
-            f2[x, y, 8:12, :] = gb2[x, y, :, 0:MAIN].astype(F32)
-            tails.append(z_slots(pad_tail(gb2[x, y, :, MAIN:CH].astype(F32)), sy))
-        t2[x, yp] = jnp.zeros((32, MAIN), F32)
-        t2[x, yp, 8:12, :] = tails[0] + tails[1]
-        return 0
-
-    lax.fori_loop(0, 18, conv2, 0)
-
-    def conv3(x, _):
-        tails = []
-        for y in range(2):
-            f3[x, 2 + y, 8:10, :] = gb3[x, y, :, 0:MAIN].astype(F32)
-            tails.append(z_slots(pad_tail(gb3[x, y, :, MAIN:CH].astype(F32)), y))
-        t3[x, 1, 8:10, :] = tails[0] + tails[1]
-        return 0
-
-    lax.fori_loop(0, 6, conv3, 0)
-
-    def build_small(i, _):
-        stx, sty, stz = i // 9, lax.rem(i // 3, 3), lax.rem(i, 3)
+            for y in range(2):
+                f3[x, 2 + y, 8:10, :] = gb3[x, y, :, 0:MAIN].astype(F32)
+                tails.append(z_slots(pad_tail(gb3[x, y, :, MAIN:CH].astype(F32)), y))
+            t3[x, 1, 8:10, :] = tails[0] + tails[1]
+
+    with jax.named_scope("conv_small"):
+        lax.fori_loop(0, 4, conv1, 0)
+        conv23()
+
+    def build_small(stx, sty, stz, store):
         row = lax.broadcasted_iota(jnp.int32, (8, MAIN), 0)
         pz = lax.rem(row, 4) + stz - 1
         inside = (pz >= 0) & (pz < 4)
@@ -314,7 +338,7 @@
         def put(j, one, two, three):
             one = [jnp.where(inside, p, 0.0) for p in one]
             rest = jnp.where(row < 2, two, jnp.where(row == 2, three, 0.0))
-            xs[i, j] = jnp.concatenate(one + [rest, z8], axis=0).astype(BF)
+            store(3 * sty + stz, j, jnp.concatenate(one + [rest, z8], axis=0).astype(BF))
 
         for sx in range(2):
             for sy in range(2):
@@ -340,86 +364,144 @@
                 + t3[2 * stx + sx, sty, pl.ds(3 + 2 * stz, 8, stride=2), :]
             )
             put(8 + sx, one, two, three)
-        return 0
-
-    lax.fori_loop(0, 27, build_small, 0)
-
-    def tails_of(kx):
-        def body(rz, _):
-            last = None
-            for ky in range(7):
-                a = pad_tail(tt[kx, ky, rz + 1])
-                b = pad_tail(tt[kx, ky, rz])
-                pair = a + pltpu.roll(b, 32, 1)
-                if last is not None:
-                    v[(kx * 6 + ky - 1) * 6 + rz] = pair + last
-                last = pltpu.roll(pair, 64, 1)
+
+    with jax.named_scope("build_small"):
+
+        def small_mid(sty, _):
+            def store(w, j, val):
+                xsm[w, j] = val
+
+            for stz in range(3):
+                build_small(1, sty, stz, store)
             return 0
 
-        lax.fori_loop(0, 6, body, 0)
-
-    def step(i, stx):
-        sty, stz = i // 3, lax.rem(i, 3)
-        t = stx * 9 + i
-        lhs = jnp.concatenate(
-            [
-                jnp.concatenate(
-                    [xb[i, j, stx : stx + 4].reshape(128, MAIN), xs[t, j]], axis=0
-                )
-                for j in range(NBLK)
-            ],
-            axis=1,
-        )
-
-        def accumulate(n, pick):
+        lax.fori_loop(0, 3, small_mid, 0)
+
+    def tail_unit(kx, rz):
+        last = None
+        for ky in range(7):
+            a = pad_tail(tt[kx, ky, rz + 1])
+            b = pad_tail(tt[kx, ky, rz])
+            pair = a + pltpu.roll(b, 32, 1)
+            if last is not None:
+                v[(kx * 6 + ky - 1) * 6 + rz] = pair + last
+            last = pltpu.roll(pair, 64, 1)
+
+    def lhs_of(stx, sty, stzs):
+        parts = []
+        for stz in stzs:
+            w = 3 * sty + stz
+            for j in range(NBLK):
+                if stx == 1:
+                    rows = [xm[w, j].reshape(128, MAIN), xsm[w, j]]
+                elif stx == 0:
+                    rows = [xe[0, w, j], xm[w, j, 0:3].reshape(96, MAIN), xse[0, w, j]]
+                else:
+                    rows = [xm[w, j, 1:4].reshape(96, MAIN), xe[1, w, j], xse[1, w, j]]
+                parts.append(jnp.concatenate(rows, axis=0))
+        return jnp.concatenate(parts, axis=1)
+
+    def dot_n(n, stx, sty, stzs):
+        blocks = []
+        for stz in stzs:
             mains = []
             tails = []
             for s in range(8):
-                w = pick(s)
-                mains.append(jnp.concatenate([x(0, MAIN) for x in w], axis=1))
-                tails.append(jnp.concatenate([x(MAIN, ROWS) for x in w], axis=1))
-            rhs = jnp.concatenate(mains + tails, axis=0)
-            res = jnp.dot(lhs, rhs, preferred_element_type=F32)
-            acc[2 * n] += res[:, 0:MAIN]
-            acc[2 * n + 1] += res[:, MAIN:]
-
-        def main_of(s, c):
-            kx = 2 * stx + (s >> 2) - (c >> 2) + 1
-            ky = 2 * sty + ((s >> 1) & 1) - ((c >> 1) & 1) + 1
-            kz = 2 * stz + (s & 1) - (c & 1) + 1
-            return lambda lo, hi: tm[kx, ky, kz, lo:hi, :]
-
-        def tail_of(s, h):
-            kx = 2 * stx + (s >> 2) - h + 1
-            ry = 2 * sty + ((s >> 1) & 1)
-            rz = 2 * stz + (s & 1)
-            k = (kx * 6 + ry) * 6 + rz
-            return lambda lo, hi: v[k, lo:hi, :]
-
+                sx, sy, sz = s >> 2, (s >> 1) & 1, s & 1
+                pair = []
+                for h in range(2):
+                    if n < 4:
+                        c = 2 * n + h
+                        kx = 2 * stx + sx - (c >> 2) + 1
+                        ky = 2 * sty + sy - ((c >> 1) & 1) + 1
+                        kz = 2 * stz + sz - (c & 1) + 1
+                        pair.append((tm[kx, ky, kz, 0:MAIN, :], tm[kx, ky, kz, MAIN:ROWS, :]))
+                    else:
+                        k = ((2 * stx + sx - h + 1) * 6 + 2 * sty + sy) * 6 + 2 * stz + sz
+                        pair.append((v[k, 0:MAIN, :], v[k, MAIN:ROWS, :]))
+                mains.append(jnp.concatenate([p[0] for p in pair], axis=1))
+                tails.append(jnp.concatenate([p[1] for p in pair], axis=1))
+            blocks += mains + tails
+        rhs = jnp.concatenate(blocks, axis=0)
+        res = jnp.dot(lhs_of(stx, sty, stzs), rhs, preferred_element_type=F32)
+        acc[2 * n] += res[:, 0:MAIN]
+        acc[2 * n + 1] += res[:, MAIN:]
+
+    def block(stx, sty, stzs, fill):
         for n in range(4):
-            accumulate(n, lambda s: [main_of(s, 2 * n), main_of(s, 2 * n + 1)])
-        accumulate(4, lambda s: [tail_of(s, 0), tail_of(s, 1)])
-
-    acc[...] = jnp.zeros(acc.shape, F32)
-    for stx, slabs in ((1, (2, 3, 4)), (0, (1, 0)), (2, (5, 6))):
+            dot_n(n, stx, sty, stzs)
+            for k in range(n * len(fill) // 4, (n + 1) * len(fill) // 4):
+                fill[k]()
+
+    def wait_t(*slabs):
         for kx in slabs:
             for c in tcopies[kx]:
                 c.wait()
-            tails_of(kx)
-        if stx == 1:
-
-            def body(i, _):
-                step(i + jnp.where(i >= 4, 1, 0), 1)
+
+    acc[...] = jnp.zeros(acc.shape, F32)
+    with jax.named_scope("wait_t"):
+        wait_t(2, 3, 4)
+    with jax.named_scope("mxu1"):
+
+        def body(i, _):
+            units = [
+                lambda kx=kx, q=q: tail_unit(kx, 3 * i + q) for q in range(3) for kx in (2, 3, 4)
+            ]
+            block(1, 2 * i, (0, 1, 2), units)
+            return 0
+
+        lax.fori_loop(0, 2, body, 0)
+
+    with jax.named_scope("wait_halo"):
+
+        @pl.when(col > 0)
+        def _():
+            rights[0].wait_recv()
+
+        @pl.when(col < n_col - 1)
+        def _():
+            lefts[0].wait_recv()
+
+    with jax.named_scope("mxu1c"):
+        fill = [lambda x=x: conv0(x) for x in (0, 1, 10, 11)]
+        for w in range(9):
+            for side in range(2):
+
+                def edge(w=w, side=side):
+                    def store(w, j, val):
+                        xe[side, w, j] = val
+
+                    build0(5 * side, w, store)
+
+                def small(w=w, side=side):
+                    def store(w, j, val):
+                        xse[side, w, j] = val
+
+                    build_small(2 * side, w // 3, w % 3, store)
+
+                fill += [edge, small]
+        block(1, 1, (0, 2), fill)
+    for stx, slabs in ((0, (1, 0)), (2, (5, 6))):
+        with jax.named_scope("wait_t"):
+            wait_t(*slabs)
+        with jax.named_scope("mxu02"):
+
+            def body(sty, _, stx=stx, slabs=slabs):
+                units = [
+                    lambda kx=kx, q=q: tail_unit(kx, 2 * sty + q) for q in range(2) for kx in slabs
+                ]
+                block(stx, sty, (0, 1, 2), units)
                 return 0
 
-            lax.fori_loop(0, 8, body, 0)
-        else:
-
-            def body(i, _, stx=stx):
-                step(i, stx)
+            lax.fori_loop(0, 3, body, 0)
+    with jax.named_scope("mxu_tail"):
+        for stx in range(3):
+
+            def body(sty, _, stx=stx):
+                dot_n(4, stx, sty, (0, 1, 2))
                 return 0
 
-            lax.fori_loop(0, 9, body, 0)
+            lax.fori_loop(0, 3, body, 0)
 
     cu_m.wait()
     cu_t.wait()
@@ -568,8 +650,10 @@
             vmem((6, 3, 32, MAIN), F32),
             vmem((6, 6, 32, MAIN), F32),
             vmem((6, 3, 32, MAIN), F32),
-            vmem((9, NBLK, 6, 32, MAIN), BF),
-            vmem((27, NBLK, 32, MAIN), BF),
+            vmem((9, NBLK, 4, 32, MAIN), BF),
+            vmem((2, 9, NBLK, 32, MAIN), BF),
+            vmem((9, NBLK, 32, MAIN), BF),
+            vmem((2, 9, NBLK, 32, MAIN), BF),
             vmem((7 * 36, ROWS, MAIN), BF),
             vmem((2, ROWS, MAIN), BF),
             vmem((NBLK, 160, MAIN), F32),

time: 54.9 us -> 43 us (0.78)
  Pallas kernels: 52.5 us -> 40.6 us
    pallas_call x1, Pallas kernels: 52.5 us -> 40.6 us  [shards(): pl.pallas_call(kernel, out_shape=jax.ShapeDtypeStruct((8, 8, 16, CH), F32...]
where the time goes in v2:
time: 43 us; the launch traced here: 42.8 us
  Pallas kernels  40.6 us (94%)
  local copies, waits for them, and re-layouts  2.26 us (5%)
    pallas_call x1, Pallas kernels, shards(): pl.pallas_call(kernel, out_shape=jax.ShapeDtypeStruct((8, 8, 16, CH), F32...  40.6 us
    unnamed x1, local copies, waits for them, and re-layouts  2.26 us

profile of v2, /device:TPU:6, one launch (start us, length us, event | category | flops | bytes accessed | tf_op | source)
XLA Modules:
  0.0 42.8 jit_solution(1134776720192987271)
XLA Ops:
  0.0 40.6 %downward.1 = f32[8,8,16,152]{3,2,1,0:T(8,128)} custom-call(bf16[8,16,16,152]{3,2,1,0:T(8,128)(2,1)} %mf.1, bf16[4,8,8,152]{3,2,1,0:T(8,128)(2,1)} %mm.1, bf16[2,4,4,152]{3,2,1,0:T(4,128)(2,1)} %mc.1, bf16[1,2,2,152]{3,2,1,0:T(2,128)(2,1)} %mt.1, bf16[7,7,7,152,152]{4,3,2,1,0:T(8,128)(2,1)} %tr.1, bf16[2,2,2,152,152]{4,3,2,1,0:T(8,128)(2,1)} %up.1), custom_call_target="tpu_custom_call" | custom-call | tf_op jit(solution)/shard_map/downward/pallas_call | solution.py:631
  40.6 2.3 %copy.8 = f32[8,8,16,152]{3,2,1,0:T(8,128)} copy(f32[8,8,16,152]{3,2,1,0:T(8,128)} %downward.1) | data formatting | bytes 1245184

commit v3 on v2

--- a/solution.py
+++ b/solution.py
@@ -24,7 +24,7 @@
     mf, mm, mc, mt, tr, up, out,
     tm, tt, um, ut, gb0, gb1, gb2, gb3,
     f0, t0, f1, t1, f2, t2, f3, t3,
-    xm, xe, xsm, xse, v, vu, acc, pm, pt, om, ot,
+    xm, xe, xsm, xse, v, v6, vu, acc, pm, pt, om, ot,
     tsem, gsem, send, recv,
 ):
     col = lax.axis_index("space")
@@ -59,7 +59,7 @@
     loc0 = pltpu.make_async_copy(mf.at[:, pl.ds(y0, 10)], gb0.at[2:10, pl.ds(d0, 10)], gsem.at[0])
     loc1 = pltpu.make_async_copy(mm.at[:, pl.ds(y1, 6)], gb1.at[2:6, pl.ds(d0, 6)], gsem.at[1])
     loc2 = pltpu.make_async_copy(mc, gb2.at[2:4, pl.ds(d0, 4)], gsem.at[2])
-    loc3 = pltpu.make_async_copy(mt, gb3.at[pl.ds(2 + odd, 1)], gsem.at[3])
+    loc3 = pltpu.make_async_copy(mt, gb3.at[3:4], gsem.at[3])
     loc0.start()
     loc1.start()
     loc2.start()
@@ -79,7 +79,7 @@
         tcopies.setdefault(kx, []).extend([a, b])
 
     idx = 0
-    for kx in (2, 3, 4, 1, 0, 5, 6):
+    for kx in (3, 2, 4, 1, 0, 5, 6):
         if 2 <= kx <= 4:
             pieces = [
                 (slice(0, 2), slice(0, 7)),
@@ -113,11 +113,13 @@
         halo(mm.at[0:2, pl.ds(y1, 6)], gb1.at[6:8, pl.ds(d0, 6)], 4, col - 1),
         halo(mc, gb2.at[4:6, pl.ds(d0, 4)], 5, col - 1),
     ]
-    top_partner = halo(mt, gb3.at[pl.ds(2 + odd, 1)], 6, base + 1 - odd)
+    top_partner = halo(mt, gb3.at[pl.ds(2 + 2 * odd, 1)], 6, base + 1 - odd)
     top_low = [
-        halo(mt, gb3.at[pl.ds(4 + odd, 1)], 7 + i, base - 2 + i, 7 + odd) for i in range(2)
+        halo(mt, gb3.at[pl.ds(5 + odd - i, 1)], 7 + i, base - 2 + i, 7 + odd) for i in range(2)
     ]
-    top_high = [halo(mt, gb3.at[pl.ds(odd, 1)], 9 + i, base + 2 + i, 9 + odd) for i in range(2)]
+    top_high = [
+        halo(mt, gb3.at[pl.ds(1 + odd - i, 1)], 9 + i, base + 2 + i, 9 + odd) for i in range(2)
+    ]
     n_greet = 1 + jnp.where(lo_ok, 2, 0) + jnp.where(hi_ok, 2, 0)
     z8 = jnp.zeros((8, MAIN), F32)
     gb0[:, pl.ds(10 * lev, 2)] = jnp.zeros((12, 2, 16, CH), BF)
@@ -136,13 +138,20 @@
         gb1[6:8] = jnp.zeros((2, 8, 8, CH), BF)
         gb2[4:6] = jnp.zeros((2, 6, 4, CH), BF)
 
+    top0 = jnp.zeros((1, 2, 2, CH), BF)
+    gb3[pl.ds(6 * odd, 1)] = top0
+
     @pl.when(par == 0)
     def _():
-        gb3[0:2] = jnp.zeros((2, 2, 2, CH), BF)
+        gb3[0:1] = top0
+        gb3[1:2] = top0
+        gb3[pl.ds(2 * (1 - odd), 1)] = top0
 
     @pl.when(par == n_col // 2 - 1)
     def _():
-        gb3[4:6] = jnp.zeros((2, 2, 2, CH), BF)
+        gb3[5:6] = top0
+        gb3[6:7] = top0
+        gb3[pl.ds(5 - odd, 1)] = top0
 
     def zero_edges(kx, _):
         for ky in range(7):
@@ -180,7 +189,7 @@
         t3[x] = jnp.zeros((3, 32, MAIN), F32)
         return 0
 
-    lax.fori_loop(0, 6, zero_coarse, 0)
+    lax.fori_loop(0, 7, zero_coarse, 0)
 
     def zero_mid(x, _):
         for sy in range(2):
@@ -234,6 +243,19 @@
 
         lax.fori_loop(2, 10, own_conv, 0)
 
+    with jax.named_scope("build_own"):
+
+        def own_build(w, _):
+            for xp in range(1, 5):
+
+                def store(w, j, val, xp=xp):
+                    xm[w, j, xp - 1] = val
+
+                build0(xp, w, store)
+            return 0
+
+        lax.fori_loop(0, 9, own_build, 0)
+
     with jax.named_scope("greet"):
         pl.semaphore_wait(barrier, n_greet)
 
@@ -259,97 +281,83 @@
             for c in lefts[::-1]:
                 c.start()
 
-    with jax.named_scope("build_own"):
-
-        def own_build(w, _):
-            for xp in range(1, 5):
-
-                def store(w, j, val, xp=xp):
-                    xm[w, j, xp - 1] = val
-
-                build0(xp, w, store)
-            return 0
-
-        lax.fori_loop(0, 9, own_build, 0)
-
-    with jax.named_scope("wait_small"):
+    def conv1(x):
+        for yp in range(4):
+            tails = []
+            for sy in range(2):
+                y = 2 * yp + sy
+                f1[x, sy, 8 + 8 * yp : 16 + 8 * yp, :] = gb1[x, y, :, 0:MAIN].astype(F32)
+                tails.append(z_slots(pad_tail(gb1[x, y, :, MAIN:CH].astype(F32)), sy))
+            t1[x, 8 + 8 * yp : 16 + 8 * yp, :] = tails[0] + tails[1]
+
+    def conv2(x):
+        for yp in range(3):
+            tails = []
+            for sy in range(2):
+                y = 2 * yp + sy
+                f2[x, y, 8:12, :] = gb2[x, y, :, 0:MAIN].astype(F32)
+                tails.append(z_slots(pad_tail(gb2[x, y, :, MAIN:CH].astype(F32)), sy))
+            t2[x, yp, 8:12, :] = tails[0] + tails[1]
+
+    def conv3(x):
+        tails = []
+        for y in range(2):
+            f3[x, 2 + y, 8:10, :] = gb3[x, y, :, 0:MAIN].astype(F32)
+            tails.append(z_slots(pad_tail(gb3[x, y, :, MAIN:CH].astype(F32)), y))
+        t3[x, 1, 8:10, :] = tails[0] + tails[1]
+
+    with jax.named_scope("conv_small"):
         loc1.wait()
         loc2.wait()
         loc3.wait()
-
-        @pl.when(col > 0)
-        def _():
-            for c in rights[1:]:
-                c.wait_recv()
-
-        @pl.when(col < n_col - 1)
-        def _():
-            for c in lefts[1:]:
-                c.wait_recv()
-
-        halo(mt, gb3.at[pl.ds(3 - odd, 1)], 6, base + 1 - odd).wait_recv()
-
-        @pl.when(lo_ok)
-        def _():
-            for i in range(2):
-                halo(mt, gb3.at[pl.ds(i, 1)], 9 + i, base - 2 + i).wait_recv()
-
-        @pl.when(hi_ok)
-        def _():
-            for i in range(2):
-                halo(mt, gb3.at[pl.ds(4 + i, 1)], 7 + i, base + 2 + i).wait_recv()
-
-    def conv1(i, _):
-        for k in range(2):
-            x = 2 * i + k
-            for yp in range(4):
-                tails = []
-                for sy in range(2):
-                    y = 2 * yp + sy
-                    f1[x, sy, 8 + 8 * yp : 16 + 8 * yp, :] = gb1[x, y, :, 0:MAIN].astype(F32)
-                    tails.append(z_slots(pad_tail(gb1[x, y, :, MAIN:CH].astype(F32)), sy))
-                t1[x, 8 + 8 * yp : 16 + 8 * yp, :] = tails[0] + tails[1]
-        return 0
-
-    def conv23():
-        for x in range(6):
-            for yp in range(3):
-                tails = []
-                for sy in range(2):
-                    y = 2 * yp + sy
-                    f2[x, y, 8:12, :] = gb2[x, y, :, 0:MAIN].astype(F32)
-                    tails.append(z_slots(pad_tail(gb2[x, y, :, MAIN:CH].astype(F32)), sy))
-                t2[x, yp, 8:12, :] = tails[0] + tails[1]
-            tails = []
-            for y in range(2):
-                f3[x, 2 + y, 8:10, :] = gb3[x, y, :, 0:MAIN].astype(F32)
-                tails.append(z_slots(pad_tail(gb3[x, y, :, MAIN:CH].astype(F32)), y))
-            t3[x, 1, 8:10, :] = tails[0] + tails[1]
-
-    with jax.named_scope("conv_small"):
-        lax.fori_loop(0, 4, conv1, 0)
-        conv23()
+        for x in range(2, 6):
+            conv1(x)
+        for x in range(2, 4):
+            conv2(x)
+        conv3(3)
 
     def build_small(stx, sty, stz, store):
         row = lax.broadcasted_iota(jnp.int32, (8, MAIN), 0)
         pz = lax.rem(row, 4) + stz - 1
         inside = (pz >= 0) & (pz < 4)
 
-        def put(j, one, two, three):
+        def put(j, one, two, three, four):
             one = [jnp.where(inside, p, 0.0) for p in one]
-            rest = jnp.where(row < 2, two, jnp.where(row == 2, three, 0.0))
+            rest = jnp.where(row < 2, two, 0.0)
+            if three is not None:
+                rest = jnp.where(row == 2, three, rest)
+            if four is not None:
+                rest = jnp.where(row == 3, four, rest)
             store(3 * sty + stz, j, jnp.concatenate(one + [rest, z8], axis=0).astype(BF))
 
         for sx in range(2):
+            three_x = {0: (1, 2), 1: (3, None), 2: (None, 6)}[stx][sx]
+            four_x = {0: (0, None), 1: (None, None), 2: (4, 5)}[stx][sx]
+
+            def top(x, y, start):
+                if x is None:
+                    return None
+                return f3[x, y, pl.ds(start + 2 * stz, 8, stride=2), :]
+
+            def top_tail(x, start):
+                if x is None:
+                    return None
+                return (
+                    t3[x, sty, pl.ds(start + 2 * stz, 8, stride=2), :]
+                    + t3[x, sty, pl.ds(start + 1 + 2 * stz, 8, stride=2), :]
+                )
+
             for sy in range(2):
                 for sz in range(2):
                     one = [
                         f1[2 * (px + stx) + sx, sy, pl.ds(6 + 8 * sty + 2 * stz + sz, 8, stride=2), :]
                         for px in range(2)
                     ]
-                    two = f2[2 * stx + sx, 2 * sty + sy, pl.ds(6 + 2 * stz + sz, 8, stride=2), :]
-                    three = f3[2 * stx + sx, 2 * sty + sy, pl.ds(2 + 2 * stz + sz, 8, stride=2), :]
-                    put(4 * sx + 2 * sy + sz, one, two, three)
+                    y = 2 * sty + sy
+                    two = f2[2 * stx + sx, y, pl.ds(6 + 2 * stz + sz, 8, stride=2), :]
+                    three = top(three_x, y, 2 + sz)
+                    four = top(four_x, y, sz)
+                    put(4 * sx + 2 * sy + sz, one, two, three, four)
             one = [
                 t1[2 * (px + stx) + sx, pl.ds(6 + 8 * sty + 2 * stz, 8, stride=2), :]
                 + t1[2 * (px + stx) + sx, pl.ds(7 + 8 * sty + 2 * stz, 8, stride=2), :]
@@ -359,11 +367,7 @@
                 t2[2 * stx + sx, sty, pl.ds(6 + 2 * stz, 8, stride=2), :]
                 + t2[2 * stx + sx, sty, pl.ds(7 + 2 * stz, 8, stride=2), :]
             )
-            three = (
-                t3[2 * stx + sx, sty, pl.ds(2 + 2 * stz, 8, stride=2), :]
-                + t3[2 * stx + sx, sty, pl.ds(3 + 2 * stz, 8, stride=2), :]
-            )
-            put(8 + sx, one, two, three)
+            put(8 + sx, one, two, top_tail(three_x, 2), top_tail(four_x, 0))
 
     with jax.named_scope("build_small"):
 
@@ -384,7 +388,10 @@
             b = pad_tail(tt[kx, ky, rz])
             pair = a + pltpu.roll(b, 32, 1)
             if last is not None:
-                v[(kx * 6 + ky - 1) * 6 + rz] = pair + last
+                if kx == 6:
+                    v6[(ky - 1) * 6 + rz] = pair + last
+                else:
+                    v[(kx * 6 + ky - 1) * 6 + rz] = pair + last
             last = pltpu.roll(pair, 64, 1)
 
     def lhs_of(stx, sty, stzs):
@@ -417,8 +424,10 @@
                         kz = 2 * stz + sz - (c & 1) + 1
                         pair.append((tm[kx, ky, kz, 0:MAIN, :], tm[kx, ky, kz, MAIN:ROWS, :]))
                     else:
-                        k = ((2 * stx + sx - h + 1) * 6 + 2 * sty + sy) * 6 + 2 * stz + sz
-                        pair.append((v[k, 0:MAIN, :], v[k, MAIN:ROWS, :]))
+                        kx = 2 * stx + sx - h + 1
+                        ref = v6 if kx == 6 else v
+                        k = ((0 if kx == 6 else 6 * kx) + 2 * sty + sy) * 6 + 2 * stz + sz
+                        pair.append((ref[k, 0:MAIN, :], ref[k, MAIN:ROWS, :]))
                 mains.append(jnp.concatenate([p[0] for p in pair], axis=1))
                 tails.append(jnp.concatenate([p[1] for p in pair], axis=1))
             blocks += mains + tails
@@ -440,30 +449,54 @@
 
     acc[...] = jnp.zeros(acc.shape, F32)
     with jax.named_scope("wait_t"):
-        wait_t(2, 3, 4)
+        wait_t(3)
+    with jax.named_scope("front"):
+
+        def front(rz, _):
+            tail_unit(3, rz)
+            return 0
+
+        lax.fori_loop(2, 6, front, 0)
+    with jax.named_scope("wait_t"):
+        wait_t(2, 4)
     with jax.named_scope("mxu1"):
 
         def body(i, _):
-            units = [
-                lambda kx=kx, q=q: tail_unit(kx, 3 * i + q) for q in range(3) for kx in (2, 3, 4)
-            ]
+            units = [lambda q=q: tail_unit(2, 3 * i + q) for q in range(3)]
+            units.append(lambda: tail_unit(3, i))
             block(1, 2 * i, (0, 1, 2), units)
             return 0
 
         lax.fori_loop(0, 2, body, 0)
 
     with jax.named_scope("wait_halo"):
-
         @pl.when(col > 0)
         def _():
-            rights[0].wait_recv()
+            for c in rights:
+                c.wait_recv()
 
         @pl.when(col < n_col - 1)
         def _():
-            lefts[0].wait_recv()
+            for c in lefts:
+                c.wait_recv()
+
+        halo(mt, gb3.at[pl.ds(4 - 2 * odd, 1)], 6, base + 1 - odd).wait_recv()
+
+        @pl.when(lo_ok)
+        def _():
+            for i in range(2):
+                halo(mt, gb3.at[pl.ds(1 + i - odd, 1)], 9 + i, base - 2 + i).wait_recv()
+
+        @pl.when(hi_ok)
+        def _():
+            for i in range(2):
+                halo(mt, gb3.at[pl.ds(5 + i - odd, 1)], 7 + i, base + 2 + i).wait_recv()
 
     with jax.named_scope("mxu1c"):
         fill = [lambda x=x: conv0(x) for x in (0, 1, 10, 11)]
+        fill += [lambda x=x: conv1(x) for x in (0, 1, 6, 7)]
+        fill += [lambda x=x: conv2(x) for x in (0, 1, 4, 5)]
+        fill += [lambda x=x: conv3(x) for x in (0, 1, 2, 4, 5, 6)]
         for w in range(9):
             for side in range(2):
 
@@ -481,24 +514,26 @@
 
                 fill += [edge, small]
         block(1, 1, (0, 2), fill)
-    for stx, slabs in ((0, (1, 0)), (2, (5, 6))):
+    for stx, slabs, extra in ((0, (1, 0), (4, 1)), (2, (5, 6), (0, 5))):
         with jax.named_scope("wait_t"):
             wait_t(*slabs)
         with jax.named_scope("mxu02"):
 
-            def body(sty, _, stx=stx, slabs=slabs):
+            def body(sty, _, stx=stx, extra=extra):
                 units = [
-                    lambda kx=kx, q=q: tail_unit(kx, 2 * sty + q) for q in range(2) for kx in slabs
+                    lambda kx=kx, q=q: tail_unit(kx, 2 * sty + q) for q in range(2) for kx in extra
                 ]
                 block(stx, sty, (0, 1, 2), units)
                 return 0
 
             lax.fori_loop(0, 3, body, 0)
     with jax.named_scope("mxu_tail"):
-        for stx in range(3):
-
-            def body(sty, _, stx=stx):
+        for stx, first in ((1, 0), (0, 3), (2, None)):
+
+            def body(sty, _, stx=stx, first=first):
                 dot_n(4, stx, sty, (0, 1, 2))
+                if first is not None:
+                    tail_unit(6, first + sty)
                 return 0
 
             lax.fori_loop(0, 3, body, 0)
@@ -549,18 +584,14 @@
     pt[...] = jnp.zeros(pt.shape, F32)
     rest = [acc[j, 144:152, :] for j in range(NBLK)]
     for cz in range(2):
-        mains = [rest[4 * a + 2 * b + cz] for a in range(2) for b in range(2)]
-        tails = [
-            tail_lanes(rest[8 + a], 4 * a + 2 * b + cz) for a in range(2) for b in range(2)
-        ]
-
-        def choose(four):
-            low = jnp.where(lev == 0, four[0], four[1])
-            high = jnp.where(lev == 0, four[2], four[3])
-            return jnp.where(odd == 0, low, high)
-
-        pm[cz : cz + 1, :] = choose(mains)[2:3]
-        pt[cz : cz + 1, :] = choose(tails)[2:3]
+        mains = []
+        tails = []
+        for cy in range(2):
+            c = 2 * cy + cz
+            mains.append(rest[c][2:3] + rest[4 + c][3:4])
+            tails.append(tail_lanes(rest[8], c)[2:3] + tail_lanes(rest[9], c)[3:4])
+        pm[cz : cz + 1, :] = jnp.where(lev == 0, mains[0], mains[1])
+        pt[cz : cz + 1, :] = jnp.where(lev == 0, tails[0], tails[1])
     add = upsampled(pm[0:16, :], pt[0:16, :])
     local2 = [rest[j] + add[j][0:8] for j in range(NBLK)]
     for c in range(8):
@@ -641,20 +672,21 @@
             vmem((12, 12, 16, CH), BF),
             vmem((8, 8, 8, CH), BF),
             vmem((6, 6, 4, CH), BF),
-            vmem((6, 2, 2, CH), BF),
+            vmem((7, 2, 2, CH), BF),
             vmem((12, 12, 32, MAIN), F32),
             vmem((12, 6, 32, MAIN), F32),
             vmem((8, 2, 48, MAIN), F32),
             vmem((8, 48, MAIN), F32),
-            vmem((6, 6, 32, MAIN), F32),
-            vmem((6, 3, 32, MAIN), F32),
-            vmem((6, 6, 32, MAIN), F32),
-            vmem((6, 3, 32, MAIN), F32),
+            vmem((7, 6, 32, MAIN), F32),
+            vmem((7, 3, 32, MAIN), F32),
+            vmem((7, 6, 32, MAIN), F32),
+            vmem((7, 3, 32, MAIN), F32),
             vmem((9, NBLK, 4, 32, MAIN), BF),
             vmem((2, 9, NBLK, 32, MAIN), BF),
             vmem((9, NBLK, 32, MAIN), BF),
             vmem((2, 9, NBLK, 32, MAIN), BF),
-            vmem((7 * 36, ROWS, MAIN), BF),
+            vmem((6 * 36, ROWS, MAIN), BF),
+            vmem((36, ROWS, MAIN), BF),
             vmem((2, ROWS, MAIN), BF),
             vmem((NBLK, 160, MAIN), F32),
             vmem((160, MAIN), F32),

time: 43 us -> 37.7 us (0.88)
  Pallas kernels: 40.6 us -> 35.3 us
    pallas_call x1, Pallas kernels: 40.6 us -> 35.3 us  [shards(): pl.pallas_call(kernel, out_shape=jax.ShapeDtypeStruct((8, 8, 16, CH), F32...]
where the time goes in v3:
time: 37.7 us; the launch traced here: 37.6 us
  Pallas kernels  35.3 us (94%)
  local copies, waits for them, and re-layouts  2.26 us (6%)
    pallas_call x1, Pallas kernels, shards(): pl.pallas_call(kernel, out_shape=jax.ShapeDtypeStruct((8, 8, 16, CH), F32...  35.3 us
    unnamed x1, local copies, waits for them, and re-layouts  2.26 us

profile of v3, /device:TPU:6, one launch (start us, length us, event | category | flops | bytes accessed | tf_op | source)
XLA Modules:
  0.0 37.6 jit_solution(14458949430949029317)
XLA Ops:
  0.0 35.3 %downward.1 = f32[8,8,16,152]{3,2,1,0:T(8,128)} custom-call(bf16[8,16,16,152]{3,2,1,0:T(8,128)(2,1)} %mf.1, bf16[4,8,8,152]{3,2,1,0:T(8,128)(2,1)} %mm.1, bf16[2,4,4,152]{3,2,1,0:T(4,128)(2,1)} %mc.1, bf16[1,2,2,152]{3,2,1,0:T(2,128)(2,1)} %mt.1, bf16[7,7,7,152,152]{4,3,2,1,0:T(8,128)(2,1)} %tr.1, bf16[2,2,2,152,152]{4,3,2,1,0:T(8,128)(2,1)} %up.1), custom_call_target="tpu_custom_call" | custom-call | tf_op jit(solution)/shard_map/downward/pallas_call | solution.py:662
  35.3 2.3 %copy.8 = f32[8,8,16,152]{3,2,1,0:T(8,128)} copy(f32[8,8,16,152]{3,2,1,0:T(8,128)} %downward.1) | data formatting | bytes 1245184

commit v4 on v3

--- a/solution.py
+++ b/solution.py
@@ -21,10 +21,10 @@
 
 
 def kernel(
-    mf, mm, mc, mt, tr, up, out,
-    tm, tt, um, ut, gb0, gb1, gb2, gb3,
+    mf, mm, mc, mt, tr, out,
+    tm, tt, gb0, gb1, gb2, gb3,
     f0, t0, f1, t1, f2, t2, f3, t3,
-    xm, xe, xsm, xse, v, v6, vu, acc, pm, pt, om, ot,
+    xm, xl, xr, xsm, xsl, xsr, v, v6, acc,
     tsem, gsem, send, recv,
 ):
     col = lax.axis_index("space")
@@ -92,11 +92,6 @@
         for ysl, zsl in pieces:
             tcopy(kx, ysl, zsl, idx)
             idx += 1
-    cu_m = pltpu.make_async_copy(up.at[:, :, :, :, 0:MAIN], um.at[:, :, :, 0:CH, :], gsem.at[4])
-    cu_t = pltpu.make_async_copy(up.at[:, :, :, :, MAIN:CH], ut.at[:, :, :, 0:CH, :], gsem.at[5])
-    cu_m.start()
-    cu_t.start()
-
     def halo(src, dst, i, dev, j=None):
         return pltpu.make_async_remote_copy(
             src_ref=src, dst_ref=dst, send_sem=send.at[i], recv_sem=recv.at[i if j is None else j],
@@ -168,9 +163,6 @@
         return 0
 
     lax.fori_loop(0, 9, zero_near, 0)
-    um[:, :, :, CH:ROWS, :] = jnp.zeros((2, 2, 2, ROWS - CH, MAIN), BF)
-    ut[:, :, :, CH:ROWS, :] = jnp.zeros((2, 2, 2, ROWS - CH, TAIL), BF)
-
     def zero_pads(x, _):
         for y in range(12):
             f0[x, y, 0:8, :] = z8
@@ -402,9 +394,9 @@
                 if stx == 1:
                     rows = [xm[w, j].reshape(128, MAIN), xsm[w, j]]
                 elif stx == 0:
-                    rows = [xe[0, w, j], xm[w, j, 0:3].reshape(96, MAIN), xse[0, w, j]]
+                    rows = [xl[w, j], xm[w, j, 0:3].reshape(96, MAIN), xsl[w, j]]
                 else:
-                    rows = [xm[w, j, 1:4].reshape(96, MAIN), xe[1, w, j], xse[1, w, j]]
+                    rows = [xm[w, j, 1:4].reshape(96, MAIN), xr[w, j], xsr[w, j]]
                 parts.append(jnp.concatenate(rows, axis=0))
         return jnp.concatenate(parts, axis=1)
 
@@ -456,18 +448,30 @@
             tail_unit(3, rz)
             return 0
 
-        lax.fori_loop(2, 6, front, 0)
+        lax.fori_loop(0, 6, front, 0)
     with jax.named_scope("wait_t"):
         wait_t(2, 4)
     with jax.named_scope("mxu1"):
 
         def body(i, _):
             units = [lambda q=q: tail_unit(2, 3 * i + q) for q in range(3)]
-            units.append(lambda: tail_unit(3, i))
+            units.append(lambda: tail_unit(4, i))
             block(1, 2 * i, (0, 1, 2), units)
             return 0
 
         lax.fori_loop(0, 2, body, 0)
+    with jax.named_scope("mxu1c"):
+        block(1, 1, (0, 2), [lambda q=q: tail_unit(4, q) for q in range(2, 6)])
+
+    def tail_dots(stx):
+        def body(sty, _):
+            dot_n(4, stx, sty, (0, 1, 2))
+            return 0
+
+        with jax.named_scope("mxu_tail"):
+            lax.fori_loop(0, 3, body, 0)
+
+    tail_dots(1)
 
     with jax.named_scope("wait_halo"):
         @pl.when(col > 0)
@@ -492,60 +496,107 @@
             for i in range(2):
                 halo(mt, gb3.at[pl.ds(5 + i - odd, 1)], 7 + i, base + 2 + i).wait_recv()
 
-    with jax.named_scope("mxu1c"):
-        fill = [lambda x=x: conv0(x) for x in (0, 1, 10, 11)]
-        fill += [lambda x=x: conv1(x) for x in (0, 1, 6, 7)]
-        fill += [lambda x=x: conv2(x) for x in (0, 1, 4, 5)]
-        fill += [lambda x=x: conv3(x) for x in (0, 1, 2, 4, 5, 6)]
-        for w in range(9):
-            for side in range(2):
-
-                def edge(w=w, side=side):
-                    def store(w, j, val):
-                        xe[side, w, j] = val
-
-                    build0(5 * side, w, store)
-
-                def small(w=w, side=side):
-                    def store(w, j, val):
-                        xse[side, w, j] = val
-
-                    build_small(2 * side, w // 3, w % 3, store)
-
-                fill += [edge, small]
-        block(1, 1, (0, 2), fill)
-    for stx, slabs, extra in ((0, (1, 0), (4, 1)), (2, (5, 6), (0, 5))):
-        with jax.named_scope("wait_t"):
-            wait_t(*slabs)
-        with jax.named_scope("mxu02"):
-
-            def body(sty, _, stx=stx, extra=extra):
-                units = [
-                    lambda kx=kx, q=q: tail_unit(kx, 2 * sty + q) for q in range(2) for kx in extra
-                ]
-                block(stx, sty, (0, 1, 2), units)
-                return 0
-
-            lax.fori_loop(0, 3, body, 0)
-    with jax.named_scope("mxu_tail"):
-        for stx, first in ((1, 0), (0, 3), (2, None)):
-
-            def body(sty, _, stx=stx, first=first):
-                dot_n(4, stx, sty, (0, 1, 2))
-                if first is not None:
-                    tail_unit(6, first + sty)
-                return 0
-
-            lax.fori_loop(0, 3, body, 0)
-
-    cu_m.wait()
-    cu_t.wait()
+    def edge(w, side):
+        def store(w, j, val):
+            (xl, xr)[side][w, j] = val
+
+        def store_small(w, j, val):
+            (xsl, xsr)[side][w, j] = val
+
+        build0(5 * side, w, store)
+        if isinstance(w, int):
+            build_small(2 * side, w // 3, w % 3, store_small)
+        else:
+            build_small(2 * side, w // 3, lax.rem(w, 3), store_small)
+
+    with jax.named_scope("edges"):
+        for x in (0, 1, 10, 11):
+            conv0(x)
+        for x in (0, 1, 6, 7):
+            conv1(x)
+        for x in (0, 1, 4, 5):
+            conv2(x)
+        for x in (0, 1, 2, 4, 5, 6):
+            conv3(x)
+
+        def left_edge(sty, _):
+            for q in range(3):
+                edge(3 * sty + q, 0)
+            return 0
+
+        lax.fori_loop(0, 3, left_edge, 0)
+    with jax.named_scope("wait_t"):
+        wait_t(1, 0)
+    with jax.named_scope("mxu02"):
+
+        def body(sty, _):
+            units = []
+            for q in range(2):
+                units.append(lambda q=q: tail_unit(1, 2 * sty + q))
+                units.append(lambda q=q: tail_unit(0, 2 * sty + q))
+            fill = []
+            for q in range(3):
+                fill.append(lambda q=q: edge(3 * sty + q, 1))
+            block(0, sty, (0, 1, 2), [units[0], fill[0], units[1], fill[1], units[2], fill[2], units[3]])
+            return 0
+
+        lax.fori_loop(0, 3, body, 0)
+    with jax.named_scope("wait_t"):
+        wait_t(5, 6)
+    with jax.named_scope("mxu02"):
+
+        def body(sty, _):
+            units = [lambda kx=kx, q=q: tail_unit(kx, 2 * sty + q) for q in range(2) for kx in (5, 6)]
+            block(2, sty, (0, 1, 2), units)
+            return 0
+
+        lax.fori_loop(0, 3, body, 0)
+
+    done_main = pltpu.make_async_copy(acc.at[0:8], out.at[0:8], gsem.at[0])
+    done_main.start()
+    tail_dots(0)
+    tail_dots(2)
+    done_tail = pltpu.make_async_copy(acc.at[8:NBLK], out.at[8:NBLK], gsem.at[1])
+    done_tail.start()
+    done_main.wait()
+    done_tail.wait()
+
+    top_partner.wait_send()
+
+    @pl.when(lo_ok)
+    def _():
+        for c in top_low:
+            c.wait_send()
+
+    @pl.when(hi_ok)
+    def _():
+        for c in top_high:
+            c.wait_send()
+
+    @pl.when(col < n_col - 1)
+    def _():
+        for c in rights:
+            c.wait_send()
+
+    @pl.when(col > 0)
+    def _():
+        for c in lefts:
+            c.wait_send()
+
+
+def finish(acc, up, out, vu, pm, pt, om, ot):
+    lev = lax.axis_index("level")
+
+    def up_rows(c, lo, hi, lane):
+        return up[c >> 2, (c >> 1) & 1, c & 1, lo:hi, lane]
+
     for h in range(2):
-        parts = [pad_tail(ut[h, q >> 1, q & 1]) for q in range(4)]
+        parts = [pad_tail(up[h, q >> 1, q & 1, :, MAIN:CH]) for q in range(4)]
         total = parts[0]
         for q in range(1, 4):
             total = total + pltpu.roll(parts[q], 32 * q, 1)
-        vu[h] = total
+        vu[h, 0:CH, :] = total
+        vu[h, CH:ROWS, :] = jnp.zeros((ROWS - CH, MAIN), BF)
 
     def upsampled(main, tail):
         rows = main.shape[0]
@@ -555,21 +606,19 @@
         both = (hi_t + pltpu.roll(tail - hi_t, 32, 1)).astype(BF)
         lhs = jnp.concatenate([hi_m, lo_m, both], axis=1)
 
-        def rhs_of(x):
-            return jnp.concatenate(
-                [x(0, MAIN), x(0, MAIN), x(MAIN, ROWS), x(MAIN, ROWS), jnp.zeros((64, MAIN), BF)],
-                axis=0,
-            )
+        def rhs_of(main, last):
+            last = jnp.concatenate([last, jnp.zeros((ROWS - CH, MAIN), BF)], axis=0)
+            return jnp.concatenate([main, main, last, last, jnp.zeros((64, MAIN), BF)], axis=0)
 
         cols = []
         for n in range(5):
             if n < 4:
                 pair = [
-                    rhs_of(lambda lo, hi, c=c: um[c >> 2, (c >> 1) & 1, c & 1, lo:hi, :])
+                    rhs_of(up_rows(c, 0, MAIN, slice(0, MAIN)), up_rows(c, MAIN, CH, slice(0, MAIN)))
                     for c in (2 * n, 2 * n + 1)
                 ]
             else:
-                pair = [rhs_of(lambda lo, hi, h=h: vu[h, lo:hi, :]) for h in range(2)]
+                pair = [rhs_of(vu[h, 0:MAIN, :], vu[h, MAIN:CH, :]) for h in range(2)]
             res = jnp.dot(lhs, jnp.concatenate(pair, axis=1), preferred_element_type=F32)
             cols += [res[:, 0:MAIN], res[:, MAIN:]]
         return cols
@@ -613,62 +662,35 @@
                 pm[pl.ds(r, 4, stride=2), :] = local1[c][q : q + 4]
                 pt[pl.ds(r, 4, stride=2), :] = tail[q : q + 4]
     add = upsampled(pm[32:160, :], pt[32:160, :])
-    for c in range(8):
-        cx, cy, cz = c >> 2, (c >> 1) & 1, c & 1
-        main = acc[c, 0:128, :] + add[c]
-        tail = tail_lanes(acc[8 + cx, 0:128, :] + add[8 + cx], c)
-        for px in range(4):
+    for px in range(4):
+        own = slice(32 * px, 32 * px + 32)
+        for c in range(8):
+            cx, cy, cz = c >> 2, (c >> 1) & 1, c & 1
+            main = acc[c, own, :] + add[c][own]
+            tail = tail_lanes(acc[8 + cx, own, :] + add[8 + cx][own], c)
             for py in range(4):
-                q = 32 * px + 8 * py
+                q = 8 * py
                 x, y = 2 * px + cx, 2 * py + cy
                 om[8 * x + y, pl.ds(cz, 8, stride=2), :] = main[q : q + 8]
                 ot[8 * x + y, pl.ds(cz, 8, stride=2), :] = tail[q : q + 8]
-
-    def emit(x, _):
-        for y in range(8):
-            out[x, y, :, 0:MAIN] = om[8 * x + y]
-            out[x, y, :, MAIN:CH] = ot[8 * x + y][:, 0:TAIL]
-        return 0
-
-    lax.fori_loop(0, 8, emit, 0)
-
-    top_partner.wait_send()
-
-    @pl.when(lo_ok)
-    def _():
-        for c in top_low:
-            c.wait_send()
-
-    @pl.when(hi_ok)
-    def _():
-        for c in top_high:
-            c.wait_send()
-
-    @pl.when(col < n_col - 1)
-    def _():
-        for c in rights:
-            c.wait_send()
-
-    @pl.when(col > 0)
-    def _():
-        for c in lefts:
-            c.wait_send()
+        for x in (2 * px, 2 * px + 1):
+            for y in range(8):
+                out[x, y, :, 0:MAIN] = om[8 * x + y]
+                out[x, y, :, MAIN:CH] = ot[8 * x + y][:, 0:TAIL]
 
 
 def shards(
     multipole_fine, multipole_mid, multipole_coarse, multipole_top, translation_ops, upsample_ops
 ):
     vmem = pltpu.VMEM
-    return pl.pallas_call(
+    far = pl.pallas_call(
         kernel,
-        out_shape=jax.ShapeDtypeStruct((8, 8, 16, CH), F32),
-        in_specs=[pl.BlockSpec(memory_space=pl.ANY)] * 6,
-        out_specs=pl.BlockSpec(memory_space=pltpu.VMEM),
+        out_shape=jax.ShapeDtypeStruct((NBLK, 160, MAIN), F32),
+        in_specs=[pl.BlockSpec(memory_space=pl.ANY)] * 5,
+        out_specs=pl.BlockSpec(memory_space=pl.ANY),
         scratch_shapes=[
             vmem((7, 7, 7, ROWS, MAIN), BF),
             vmem((7, 7, 7, ROWS, TAIL), BF),
-            vmem((2, 2, 2, ROWS, MAIN), BF),
-            vmem((2, 2, 2, ROWS, TAIL), BF),
             vmem((12, 12, 16, CH), BF),
             vmem((8, 8, 8, CH), BF),
             vmem((6, 6, 4, CH), BF),
@@ -682,17 +704,14 @@
             vmem((7, 6, 32, MAIN), F32),
             vmem((7, 3, 32, MAIN), F32),
             vmem((9, NBLK, 4, 32, MAIN), BF),
-            vmem((2, 9, NBLK, 32, MAIN), BF),
             vmem((9, NBLK, 32, MAIN), BF),
-            vmem((2, 9, NBLK, 32, MAIN), BF),
+            vmem((9, NBLK, 32, MAIN), BF),
+            vmem((9, NBLK, 32, MAIN), BF),
+            vmem((9, NBLK, 32, MAIN), BF),
+            vmem((9, NBLK, 32, MAIN), BF),
             vmem((6 * 36, ROWS, MAIN), BF),
             vmem((36, ROWS, MAIN), BF),
-            vmem((2, ROWS, MAIN), BF),
             vmem((NBLK, 160, MAIN), F32),
-            vmem((160, MAIN), F32),
-            vmem((160, MAIN), F32),
-            vmem((64, 16, MAIN), F32),
-            vmem((64, 16, MAIN), F32),
             pltpu.SemaphoreType.DMA((32,)),
             pltpu.SemaphoreType.DMA((6,)),
             pltpu.SemaphoreType.DMA((11,)),
@@ -702,7 +721,21 @@
             collective_id=0, has_side_effects=True, vmem_limit_bytes=66_000_000
         ),
         name="downward",
-    )(multipole_fine, multipole_mid, multipole_coarse, multipole_top, translation_ops, upsample_ops)
+    )(multipole_fine, multipole_mid, multipole_coarse, multipole_top, translation_ops)
+    return pl.pallas_call(
+        finish,
+        out_shape=jax.ShapeDtypeStruct((8, 8, 16, CH), F32),
+        in_specs=[pl.BlockSpec(memory_space=pltpu.VMEM)] * 2,
+        out_specs=pl.BlockSpec(memory_space=pltpu.VMEM),
+        scratch_shapes=[
+            vmem((2, ROWS, MAIN), BF),
+            vmem((160, MAIN), F32),
+            vmem((160, MAIN), F32),
+            vmem((64, 16, MAIN), F32),
+            vmem((64, 16, MAIN), F32),
+        ],
+        name="upsample",
+    )(far, upsample_ops)
 
 
 def solution(mesh):

time: 37.7 us -> 35.5 us (0.942)
  local copies, waits for them, and re-layouts: 2.26 us -> 0 us
    unnamed x1 -> x0, local copies, waits for them, and re-layouts: 2.26 us -> none
    pallas_call x1 -> x2, Pallas kernels: 35.3 us -> 35.4 us  [the longest x1 31.8 us: shards(): pl.pallas_call(kernel, out_shape=jax.ShapeDtypeStruct((NBLK, 160, MAIN),...]
where the time goes in v4:
time: 35.5 us; the launch traced here: 35.4 us
  Pallas kernels  35.4 us (100%)
    pallas_call x1, Pallas kernels, shards(): pl.pallas_call(kernel, out_shape=jax.ShapeDtypeStruct((NBLK, 160, MAIN),...  31.8 us
    pallas_call x1, Pallas kernels, shards(): pl.pallas_call(finish, out_shape=jax.ShapeDtypeStruct((8, 8, 16, CH), F32...  3.62 us

profile of v4, /device:TPU:6, one launch (start us, length us, event | category | flops | bytes accessed | tf_op | source)
XLA Modules:
  0.0 35.4 jit_solution(15198874895328221527)
XLA Ops:
  0.0 31.8 %downward.1.acc = f32[10,160,128]{2,1,0:T(8,128)} custom-call(bf16[8,16,16,152]{3,2,1,0:T(8,128)(2,1)} %mf.1, bf16[4,8,8,152]{3,2,1,0:T(8,128)(2,1)} %mm.1, bf16[2,4,4,152]{3,2,1,0:T(4,128)(2,1)} %mc.1, bf16[1,2,2,152]{3,2,1,0:T(2,128)(2,1)} %mt.1, bf16[7,7,7,152,152]{4,3,2,1,0:T(8,128)(2,1)} %tr.1), custom_call_target="tpu_custom_call" | custom-call | tf_op jit(solution)/shard_map/downward/pallas_call | solution.py:686
  31.8 3.6 %upsample.1 = f32[8,8,16,152]{3,2,1,0:T(8,128)} custom-call(f32[10,160,128]{2,1,0:T(8,128)} %downward.1.acc, bf16[2,2,2,152,152]{4,3,2,1,0:T(8,128)(2,1)} %up.1), custom_call_target="tpu_custom_call" | custom-call | tf_op jit(solution)/shard_map/upsample/pallas_call | solution.py:725

commit v5 on v4

--- a/solution.py
+++ b/solution.py
@@ -21,10 +21,10 @@
 
 
 def kernel(
-    mf, mm, mc, mt, tr, out,
+    mf, mm, mc, mt, tr, acc,
     tm, tt, gb0, gb1, gb2, gb3,
     f0, t0, f1, t1, f2, t2, f3, t3,
-    xm, xl, xr, xsm, xsl, xsr, v, v6, acc,
+    xm, xl, xr, xsm, xsl, xsr, v,
     tsem, gsem, send, recv,
 ):
     col = lax.axis_index("space")
@@ -248,31 +248,6 @@
 
         lax.fori_loop(0, 9, own_build, 0)
 
-    with jax.named_scope("greet"):
-        pl.semaphore_wait(barrier, n_greet)
-
-        top_partner.start()
-
-        @pl.when(lo_ok)
-        def _():
-            for c in top_low:
-                c.start()
-
-        @pl.when(hi_ok)
-        def _():
-            for c in top_high:
-                c.start()
-
-        @pl.when(col < n_col - 1)
-        def _():
-            for c in rights[::-1]:
-                c.start()
-
-        @pl.when(col > 0)
-        def _():
-            for c in lefts[::-1]:
-                c.start()
-
     def conv1(x):
         for yp in range(4):
             tails = []
@@ -323,20 +298,29 @@
             store(3 * sty + stz, j, jnp.concatenate(one + [rest, z8], axis=0).astype(BF))
 
         for sx in range(2):
-            three_x = {0: (1, 2), 1: (3, None), 2: (None, 6)}[stx][sx]
-            four_x = {0: (0, None), 1: (None, None), 2: (4, 5)}[stx][sx]
-
-            def top(x, y, start):
+            if isinstance(stx, int):
+                three_x, four_x = ((3, None)[sx], None)
+                keep = None
+            else:
+                three_x = 1 if sx == 0 else 2 + 2 * stx
+                four_x = 2 * stx if sx == 0 else 5
+                keep = (stx == 0) if sx == 0 else (stx == 2)
+
+            def only(val, wanted):
+                return val if keep is None or not wanted else jnp.where(keep, val, 0.0)
+
+            def top(x, y, start, wanted):
                 if x is None:
                     return None
-                return f3[x, y, pl.ds(start + 2 * stz, 8, stride=2), :]
-
-            def top_tail(x, start):
+                return only(f3[x, y, pl.ds(start + 2 * stz, 8, stride=2), :], wanted)
+
+            def top_tail(x, start, wanted):
                 if x is None:
                     return None
-                return (
+                return only(
                     t3[x, sty, pl.ds(start + 2 * stz, 8, stride=2), :]
-                    + t3[x, sty, pl.ds(start + 1 + 2 * stz, 8, stride=2), :]
+                    + t3[x, sty, pl.ds(start + 1 + 2 * stz, 8, stride=2), :],
+                    wanted,
                 )
 
             for sy in range(2):
@@ -347,8 +331,8 @@
                     ]
                     y = 2 * sty + sy
                     two = f2[2 * stx + sx, y, pl.ds(6 + 2 * stz + sz, 8, stride=2), :]
-                    three = top(three_x, y, 2 + sz)
-                    four = top(four_x, y, sz)
+                    three = top(three_x, y, 2 + sz, sx == 0)
+                    four = top(four_x, y, sz, sx == 1)
                     put(4 * sx + 2 * sy + sz, one, two, three, four)
             one = [
                 t1[2 * (px + stx) + sx, pl.ds(6 + 8 * sty + 2 * stz, 8, stride=2), :]
@@ -359,7 +343,7 @@
                 t2[2 * stx + sx, sty, pl.ds(6 + 2 * stz, 8, stride=2), :]
                 + t2[2 * stx + sx, sty, pl.ds(7 + 2 * stz, 8, stride=2), :]
             )
-            put(8 + sx, one, two, top_tail(three_x, 2), top_tail(four_x, 0))
+            put(8 + sx, one, two, top_tail(three_x, 2, sx == 0), top_tail(four_x, 0, sx == 1))
 
     with jax.named_scope("build_small"):
 
@@ -380,11 +364,47 @@
             b = pad_tail(tt[kx, ky, rz])
             pair = a + pltpu.roll(b, 32, 1)
             if last is not None:
-                if kx == 6:
-                    v6[(ky - 1) * 6 + rz] = pair + last
-                else:
-                    v[(kx * 6 + ky - 1) * 6 + rz] = pair + last
+                v[(kx * 6 + ky - 1) * 6 + rz] = pair + last
             last = pltpu.roll(pair, 64, 1)
+
+    def wait_t(*slabs):
+        for kx in slabs:
+            for c in tcopies[kx]:
+                c.wait()
+
+    with jax.named_scope("wait_t"):
+        wait_t(3)
+    with jax.named_scope("front"):
+
+        def front(rz, _):
+            tail_unit(3, rz)
+            return 0
+
+        pass
+    with jax.named_scope("greet"):
+        pl.semaphore_wait(barrier, n_greet)
+
+        top_partner.start()
+
+        @pl.when(lo_ok)
+        def _():
+            for c in top_low:
+                c.start()
+
+        @pl.when(hi_ok)
+        def _():
+            for c in top_high:
+                c.start()
+
+        @pl.when((col < n_col - 1) & (lev == 0))
+        def _():
+            for c in rights[::-1]:
+                c.start()
+
+        @pl.when((col > 0) & (lev == 1))
+        def _():
+            for c in lefts[::-1]:
+                c.start()
 
     def lhs_of(stx, sty, stzs):
         parts = []
@@ -393,15 +413,20 @@
             for j in range(NBLK):
                 if stx == 1:
                     rows = [xm[w, j].reshape(128, MAIN), xsm[w, j]]
-                elif stx == 0:
-                    rows = [xl[w, j], xm[w, j, 0:3].reshape(96, MAIN), xsl[w, j]]
-                else:
-                    rows = [xm[w, j, 1:4].reshape(96, MAIN), xr[w, j], xsr[w, j]]
+                elif isinstance(stx, tuple):
+                    k, side = stx
+                    mid = xm[w, j, pl.ds(side, 3)].reshape(96, MAIN)
+                    rows = [(xl, xr)[k][w, j], mid, (xsl, xsr)[k][w, j]]
                 parts.append(jnp.concatenate(rows, axis=0))
         return jnp.concatenate(parts, axis=1)
 
     def dot_n(n, stx, sty, stzs):
         blocks = []
+        lhs = lhs_of(stx, sty, stzs)
+        two_sided = isinstance(stx, tuple)
+        if two_sided:
+            side = stx[1]
+            stx = 2 * side
         for stz in stzs:
             mains = []
             tails = []
@@ -416,17 +441,21 @@
                         kz = 2 * stz + sz - (c & 1) + 1
                         pair.append((tm[kx, ky, kz, 0:MAIN, :], tm[kx, ky, kz, MAIN:ROWS, :]))
                     else:
-                        kx = 2 * stx + sx - h + 1
-                        ref = v6 if kx == 6 else v
-                        k = ((0 if kx == 6 else 6 * kx) + 2 * sty + sy) * 6 + 2 * stz + sz
-                        pair.append((ref[k, 0:MAIN, :], ref[k, MAIN:ROWS, :]))
+                        k = ((2 * stx + sx - h + 1) * 6 + 2 * sty + sy) * 6 + 2 * stz + sz
+                        pair.append((v[k, 0:MAIN, :], v[k, MAIN:ROWS, :]))
                 mains.append(jnp.concatenate([p[0] for p in pair], axis=1))
                 tails.append(jnp.concatenate([p[1] for p in pair], axis=1))
             blocks += mains + tails
         rhs = jnp.concatenate(blocks, axis=0)
-        res = jnp.dot(lhs_of(stx, sty, stzs), rhs, preferred_element_type=F32)
-        acc[2 * n] += res[:, 0:MAIN]
-        acc[2 * n + 1] += res[:, MAIN:]
+        res = jnp.dot(lhs, rhs, preferred_element_type=F32)
+        for h in range(2):
+            own = res[:, MAIN * h : MAIN * (h + 1)]
+            if two_sided:
+                acc[2 * n + h, pl.ds(pl.multiple_of(96 * side, 32), 32)] += own[0:32]
+                acc[2 * n + h, pl.ds(pl.multiple_of(32 - 32 * side, 32), 96)] += own[32:128]
+                acc[2 * n + h, 128:160] += own[128:160]
+            else:
+                acc[2 * n + h] += own
 
     def block(stx, sty, stzs, fill):
         for n in range(4):
@@ -434,21 +463,9 @@
             for k in range(n * len(fill) // 4, (n + 1) * len(fill) // 4):
                 fill[k]()
 
-    def wait_t(*slabs):
-        for kx in slabs:
-            for c in tcopies[kx]:
-                c.wait()
-
+    with jax.named_scope("front"):
+        lax.fori_loop(0, 6, front, 0)
     acc[...] = jnp.zeros(acc.shape, F32)
-    with jax.named_scope("wait_t"):
-        wait_t(3)
-    with jax.named_scope("front"):
-
-        def front(rz, _):
-            tail_unit(3, rz)
-            return 0
-
-        lax.fori_loop(0, 6, front, 0)
     with jax.named_scope("wait_t"):
         wait_t(2, 4)
     with jax.named_scope("mxu1"):
@@ -460,6 +477,17 @@
             return 0
 
         lax.fori_loop(0, 2, body, 0)
+
+    @pl.when((col < n_col - 1) & (lev == 1))
+    def _():
+        for c in rights[::-1]:
+            c.start()
+
+    @pl.when((col > 0) & (lev == 0))
+    def _():
+        for c in lefts[::-1]:
+            c.start()
+
     with jax.named_scope("mxu1c"):
         block(1, 1, (0, 2), [lambda q=q: tail_unit(4, q) for q in range(2, 6)])
 
@@ -474,92 +502,99 @@
     tail_dots(1)
 
     with jax.named_scope("wait_halo"):
-        @pl.when(col > 0)
+
+        halo(mt, gb3.at[pl.ds(4 - 2 * odd, 1)], 6, base + 1 - odd).wait_recv()
+
+        @pl.when(lo_ok)
+        def _():
+            for i in range(2):
+                halo(mt, gb3.at[pl.ds(1 + i - odd, 1)], 9 + i, base - 2 + i).wait_recv()
+
+        @pl.when(hi_ok)
+        def _():
+            for i in range(2):
+                halo(mt, gb3.at[pl.ds(5 + i - odd, 1)], 7 + i, base + 2 + i).wait_recv()
+
+        @pl.when((col > 0) & (lev == 0))
         def _():
             for c in rights:
                 c.wait_recv()
 
-        @pl.when(col < n_col - 1)
+        @pl.when((col < n_col - 1) & (lev == 1))
         def _():
             for c in lefts:
                 c.wait_recv()
 
-        halo(mt, gb3.at[pl.ds(4 - 2 * odd, 1)], 6, base + 1 - odd).wait_recv()
-
-        @pl.when(lo_ok)
-        def _():
-            for i in range(2):
-                halo(mt, gb3.at[pl.ds(1 + i - odd, 1)], 9 + i, base - 2 + i).wait_recv()
-
-        @pl.when(hi_ok)
-        def _():
-            for i in range(2):
-                halo(mt, gb3.at[pl.ds(5 + i - odd, 1)], 7 + i, base + 2 + i).wait_recv()
-
-    def edge(w, side):
+    one_side = lev
+    two_side = 1 - lev
+
+    def convert(side):
+        for x in range(2):
+            conv0(10 * side + x)
+            conv1(6 * side + x)
+            conv2(4 * side + x)
+        for x in range(3):
+            conv3(4 * side + x)
+
+    def edge(w, side, k):
         def store(w, j, val):
-            (xl, xr)[side][w, j] = val
+            (xl, xr)[k][w, j] = val
 
         def store_small(w, j, val):
-            (xsl, xsr)[side][w, j] = val
+            (xsl, xsr)[k][w, j] = val
 
         build0(5 * side, w, store)
-        if isinstance(w, int):
-            build_small(2 * side, w // 3, w % 3, store_small)
-        else:
-            build_small(2 * side, w // 3, lax.rem(w, 3), store_small)
+        build_small(2 * side, w // 3, lax.rem(w, 3), store_small)
 
     with jax.named_scope("edges"):
-        for x in (0, 1, 10, 11):
-            conv0(x)
-        for x in (0, 1, 6, 7):
-            conv1(x)
-        for x in (0, 1, 4, 5):
-            conv2(x)
-        for x in (0, 1, 2, 4, 5, 6):
-            conv3(x)
-
-        def left_edge(sty, _):
+        convert(one_side)
+
+        def first_edge(sty, _):
             for q in range(3):
-                edge(3 * sty + q, 0)
+                edge(3 * sty + q, one_side, 0)
             return 0
 
-        lax.fori_loop(0, 3, left_edge, 0)
+        lax.fori_loop(0, 3, first_edge, 0)
     with jax.named_scope("wait_t"):
-        wait_t(1, 0)
+        wait_t(1, 0, 5, 6)
+
+    def units_of(sty, slabs):
+        return [lambda kx=kx, q=q: tail_unit(kx, 2 * sty + q) for q in range(2) for kx in slabs]
+
+    def side_body(k, side, more):
+        def body(sty, _):
+            fill = units_of(sty, (1, 0) if k == 0 else (5, 6))
+            for q in range(more):
+                fill.append(lambda q=q: edge(more * sty - more + q, two_side, 1))
+            block((k, side), sty, (0, 1, 2), fill)
+            return 0
+
+        return body
+
     with jax.named_scope("mxu02"):
-
-        def body(sty, _):
-            units = []
-            for q in range(2):
-                units.append(lambda q=q: tail_unit(1, 2 * sty + q))
-                units.append(lambda q=q: tail_unit(0, 2 * sty + q))
-            fill = []
-            for q in range(3):
-                fill.append(lambda q=q: edge(3 * sty + q, 1))
-            block(0, sty, (0, 1, 2), [units[0], fill[0], units[1], fill[1], units[2], fill[2], units[3]])
-            return 0
-
-        lax.fori_loop(0, 3, body, 0)
-    with jax.named_scope("wait_t"):
-        wait_t(5, 6)
+        lax.fori_loop(0, 1, side_body(0, one_side, 0), 0)
+    with jax.named_scope("wait_halo"):
+
+        @pl.when((col > 0) & (lev == 1))
+        def _():
+            for c in rights:
+                c.wait_recv()
+
+        @pl.when((col < n_col - 1) & (lev == 0))
+        def _():
+            for c in lefts:
+                c.wait_recv()
+
+    with jax.named_scope("edges"):
+        convert(two_side)
     with jax.named_scope("mxu02"):
-
-        def body(sty, _):
-            units = [lambda kx=kx, q=q: tail_unit(kx, 2 * sty + q) for q in range(2) for kx in (5, 6)]
-            block(2, sty, (0, 1, 2), units)
-            return 0
-
-        lax.fori_loop(0, 3, body, 0)
-
-    done_main = pltpu.make_async_copy(acc.at[0:8], out.at[0:8], gsem.at[0])
-    done_main.start()
-    tail_dots(0)
-    tail_dots(2)
-    done_tail = pltpu.make_async_copy(acc.at[8:NBLK], out.at[8:NBLK], gsem.at[1])
-    done_tail.start()
-    done_main.wait()
-    done_tail.wait()
+        lax.fori_loop(1, 3, side_body(0, one_side, 4), 0)
+    edge(jnp.int32(8), two_side, 1)
+    with jax.named_scope("mxu02"):
+        lax.fori_loop(0, 3, side_body(1, two_side, 0), 0)
+
+    tail_dots((0, one_side))
+    tail_dots((1, two_side))
 
     top_partner.wait_send()
 
@@ -584,9 +619,8 @@
             c.wait_send()
 
 
-def finish(acc, up, out, vu, pm, pt, om, ot):
+def finish(acc, up, out, vu, pm, pt, om, ot, ob, osem):
     lev = lax.axis_index("level")
-
     def up_rows(c, lo, hi, lane):
         return up[c >> 2, (c >> 1) & 1, c & 1, lo:hi, lane]
 
@@ -662,6 +696,7 @@
                 pm[pl.ds(r, 4, stride=2), :] = local1[c][q : q + 4]
                 pt[pl.ds(r, 4, stride=2), :] = tail[q : q + 4]
     add = upsampled(pm[32:160, :], pt[32:160, :])
+    stores = []
     for px in range(4):
         own = slice(32 * px, 32 * px + 32)
         for c in range(8):
@@ -675,8 +710,13 @@
                 ot[8 * x + y, pl.ds(cz, 8, stride=2), :] = tail[q : q + 8]
         for x in (2 * px, 2 * px + 1):
             for y in range(8):
-                out[x, y, :, 0:MAIN] = om[8 * x + y]
-                out[x, y, :, MAIN:CH] = ot[8 * x + y][:, 0:TAIL]
+                ob[x, y, :, 0:MAIN] = om[8 * x + y]
+                ob[x, y, :, MAIN:CH] = ot[8 * x + y][:, 0:TAIL]
+        pair = pl.ds(2 * px, 2)
+        stores.append(pltpu.make_async_copy(ob.at[pair], out.at[pair], osem.at[px]))
+        stores[-1].start()
+    for c in stores:
+        c.wait()
 
 
 def shards(
@@ -685,9 +725,9 @@
     vmem = pltpu.VMEM
     far = pl.pallas_call(
         kernel,
-        out_shape=jax.ShapeDtypeStruct((NBLK, 160, MAIN), F32),
-        in_specs=[pl.BlockSpec(memory_space=pl.ANY)] * 5,
-        out_specs=pl.BlockSpec(memory_space=pl.ANY),
+        out_shape=pltpu.VMEM((NBLK, 160, MAIN), F32),
+        in_specs=[pl.BlockSpec(memory_space=pltpu.HBM)] * 5,
+        out_specs=pl.BlockSpec(memory_space=pltpu.VMEM),
         scratch_shapes=[
             vmem((7, 7, 7, ROWS, MAIN), BF),
             vmem((7, 7, 7, ROWS, TAIL), BF),
@@ -709,16 +749,14 @@
             vmem((9, NBLK, 32, MAIN), BF),
             vmem((9, NBLK, 32, MAIN), BF),
             vmem((9, NBLK, 32, MAIN), BF),
-            vmem((6 * 36, ROWS, MAIN), BF),
-            vmem((36, ROWS, MAIN), BF),
-            vmem((NBLK, 160, MAIN), F32),
+            vmem((7 * 36, ROWS, MAIN), BF),
             pltpu.SemaphoreType.DMA((32,)),
             pltpu.SemaphoreType.DMA((6,)),
             pltpu.SemaphoreType.DMA((11,)),
             pltpu.SemaphoreType.DMA((11,)),
         ],
         compiler_params=pltpu.CompilerParams(
-            collective_id=0, has_side_effects=True, vmem_limit_bytes=66_000_000
+            collective_id=0, has_side_effects=True, vmem_limit_bytes=56_000_000
         ),
         name="downward",
     )(multipole_fine, multipole_mid, multipole_coarse, multipole_top, translation_ops)
@@ -726,14 +764,17 @@
         finish,
         out_shape=jax.ShapeDtypeStruct((8, 8, 16, CH), F32),
         in_specs=[pl.BlockSpec(memory_space=pltpu.VMEM)] * 2,
-        out_specs=pl.BlockSpec(memory_space=pltpu.VMEM),
+        out_specs=pl.BlockSpec(memory_space=pl.ANY),
         scratch_shapes=[
             vmem((2, ROWS, MAIN), BF),
             vmem((160, MAIN), F32),
             vmem((160, MAIN), F32),
             vmem((64, 16, MAIN), F32),
             vmem((64, 16, MAIN), F32),
+            vmem((8, 8, 16, CH), F32),
+            pltpu.SemaphoreType.DMA((4,)),
         ],
+        compiler_params=pltpu.CompilerParams(vmem_limit_bytes=24_000_000),
         name="upsample",
     )(far, upsample_ops)
 

time: 35.5 us -> 34.3 us (0.966); the launches traced: 35.4 us -> 33.8 us
  Pallas kernels: 35.4 us -> 33.8 us
    pallas_call x1, Pallas kernels: 3.62 us -> 2.19 us  [shards(): pl.pallas_call(finish, out_shape=jax.ShapeDtypeStruct((8, 8, 16, CH), F32...]
where the time goes in v5:
time: 34.3 us; the launch traced here: 33.8 us
  Pallas kernels  33.8 us (99%)
    pallas_call x1, Pallas kernels, shards(): pl.pallas_call(kernel, out_shape=pltpu.VMEM((NBLK, 160, MAIN), F32), in_s...  31.6 us
    pallas_call x1, Pallas kernels, shards(): pl.pallas_call(finish, out_shape=jax.ShapeDtypeStruct((8, 8, 16, CH), F32...  2.19 us

profile of v5, /device:TPU:6, one launch (start us, length us, event | category | flops | bytes accessed | tf_op | source)
XLA Modules:
  0.0 33.8 jit_solution(13080700197745511232)
XLA Ops:
  0.0 0.0 copy-start
  0.0 31.6 %downward.1.acc = f32[10,160,128]{2,1,0:T(8,128)S(1)} custom-call(bf16[8,16,16,152]{3,2,1,0:T(8,128)(2,1)} %mf.1, bf16[4,8,8,152]{3,2,1,0:T(8,128)(2,1)} %mm.1, bf16[2,4,4,152]{3,2,1,0:T(4,128)(2,1)} %mc.1, bf16[1,2,2,152]{3,2,1,0:T(2,128)(2,1)} %mt.1, bf16[7,7,7,152,152]{4,3,2,1,0:T(8,128)(2,1)} %tr.1), custom_call_target="tpu_custom_call" | custom-call | tf_op jit(solution)/shard_map/downward/pallas_call | solution.py:726
  31.6 0.0 copy-done
  31.6 2.2 %upsample.1 = f32[8,8,16,152]{3,2,1,0:T(8,128)} custom-call(f32[10,160,128]{2,1,0:T(8,128)S(1)} %downward.1.acc, bf16[2,2,2,152,152]{4,3,2,1,0:T(8,128)(2,1)S(1)} %copy-done), custom_call_target="tpu_custom_call" | custom-call | tf_op jit(solution)/shard_map/upsample/pallas_call | solution.py:763
Async XLA Ops:
  0.0 31.6 %copy-start = (bf16[2,2,2,152,152]{4,3,2,1,0:T(8,128)(2,1)S(1)}, bf16[2,2,2,152,152]{4,3,2,1,0:T(8,128)(2,1)}, u32[]{:S(2)}) copy-start(bf16[2,2,2,152,152]{4,3,2,1,0:T(8,128)(2,1)} %up.1) | copy-start | bytes 1108996

commit v6 on v5

--- a/solution.py
+++ b/solution.py
@@ -156,13 +156,6 @@
 
     lax.fori_loop(0, 7, zero_edges, 0)
 
-    def zero_near(i, _):
-        for kz in range(2, 5):
-            tm[2 + i // 3, 2 + lax.rem(i, 3), kz, 0:CH, :] = jnp.zeros((CH, MAIN), BF)
-            tt[2 + i // 3, 2 + lax.rem(i, 3), kz, 0:CH, :] = jnp.zeros((CH, TAIL), BF)
-        return 0
-
-    lax.fori_loop(0, 9, zero_near, 0)
     def zero_pads(x, _):
         for y in range(12):
             f0[x, y, 0:8, :] = z8
@@ -272,16 +265,6 @@
             f3[x, 2 + y, 8:10, :] = gb3[x, y, :, 0:MAIN].astype(F32)
             tails.append(z_slots(pad_tail(gb3[x, y, :, MAIN:CH].astype(F32)), y))
         t3[x, 1, 8:10, :] = tails[0] + tails[1]
-
-    with jax.named_scope("conv_small"):
-        loc1.wait()
-        loc2.wait()
-        loc3.wait()
-        for x in range(2, 6):
-            conv1(x)
-        for x in range(2, 4):
-            conv2(x)
-        conv3(3)
 
     def build_small(stx, sty, stz, store):
         row = lax.broadcasted_iota(jnp.int32, (8, MAIN), 0)
@@ -345,18 +328,6 @@
             )
             put(8 + sx, one, two, top_tail(three_x, 2, sx == 0), top_tail(four_x, 0, sx == 1))
 
-    with jax.named_scope("build_small"):
-
-        def small_mid(sty, _):
-            def store(w, j, val):
-                xsm[w, j] = val
-
-            for stz in range(3):
-                build_small(1, sty, stz, store)
-            return 0
-
-        lax.fori_loop(0, 3, small_mid, 0)
-
     def tail_unit(kx, rz):
         last = None
         for ky in range(7):
@@ -372,94 +343,135 @@
             for c in tcopies[kx]:
                 c.wait()
 
+    with jax.named_scope("greet"):
+        pl.semaphore_wait(barrier, n_greet)
+
+        top_partner.start()
+
+        @pl.when(lo_ok)
+        def _():
+            for c in top_low:
+                c.start()
+
+        @pl.when(hi_ok)
+        def _():
+            for c in top_high:
+                c.start()
+
+        @pl.when((col < n_col - 1) & (lev == 0))
+        def _():
+            for c in rights[::-1]:
+                c.start()
+
+        @pl.when((col > 0) & (lev == 1))
+        def _():
+            for c in lefts[::-1]:
+                c.start()
+
+    def zero_near(i, _):
+        for kz in range(2, 5):
+            tm[2 + i // 3, 2 + lax.rem(i, 3), kz, 0:CH, :] = jnp.zeros((CH, MAIN), BF)
+            tt[2 + i // 3, 2 + lax.rem(i, 3), kz, 0:CH, :] = jnp.zeros((CH, TAIL), BF)
+        return 0
+
+    lax.fori_loop(0, 9, zero_near, 0)
+    with jax.named_scope("conv_small"):
+        loc1.wait()
+        loc2.wait()
+        loc3.wait()
+        for x in range(2, 6):
+            conv1(x)
+        for x in range(2, 4):
+            conv2(x)
+        conv3(3)
+
+    with jax.named_scope("build_small"):
+
+        def small_mid(sty, _):
+            def store(w, j, val):
+                xsm[w, j] = val
+
+            for stz in range(3):
+                build_small(1, sty, stz, store)
+            return 0
+
+        lax.fori_loop(0, 3, small_mid, 0)
+
     with jax.named_scope("wait_t"):
         wait_t(3)
-    with jax.named_scope("front"):
-
-        def front(rz, _):
-            tail_unit(3, rz)
-            return 0
-
-        pass
-    with jax.named_scope("greet"):
-        pl.semaphore_wait(barrier, n_greet)
-
-        top_partner.start()
-
-        @pl.when(lo_ok)
-        def _():
-            for c in top_low:
-                c.start()
-
-        @pl.when(hi_ok)
-        def _():
-            for c in top_high:
-                c.start()
-
-        @pl.when((col < n_col - 1) & (lev == 0))
-        def _():
-            for c in rights[::-1]:
-                c.start()
-
-        @pl.when((col > 0) & (lev == 1))
-        def _():
-            for c in lefts[::-1]:
-                c.start()
-
-    def lhs_of(stx, sty, stzs):
+
+    def front(rz, _):
+        tail_unit(3, rz)
+        return 0
+
+    def lhs_part(stx, w, j):
+        if isinstance(stx, tuple):
+            k, side = stx
+            mid = xm[w, j, pl.ds(side, 3)].reshape(96, MAIN)
+            rows = [(xl, xr)[k][w, j], mid, (xsl, xsr)[k][w, j]]
+        else:
+            rows = [xm[w, j].reshape(128, MAIN), xsm[w, j]]
+        return jnp.concatenate(rows, axis=0)
+
+    def near(step, s, c):
+        return all(
+            abs(2 * t - 2 + ((s >> b) & 1) - ((c >> b) & 1)) <= 1 for t, b in zip(step, (2, 1, 0))
+        )
+
+    def dot_n(cs, stx, sty, stzs, order=(0, 1, 2, 3, 4, 5, 6, 7)):
+        two_sided = isinstance(stx, tuple)
+        step_x = 2 * stx[1] if two_sided else stx
         parts = []
+        blocks = []
         for stz in stzs:
             w = 3 * sty + stz
-            for j in range(NBLK):
-                if stx == 1:
-                    rows = [xm[w, j].reshape(128, MAIN), xsm[w, j]]
-                elif isinstance(stx, tuple):
-                    k, side = stx
-                    mid = xm[w, j, pl.ds(side, 3)].reshape(96, MAIN)
-                    rows = [(xl, xr)[k][w, j], mid, (xsl, xsr)[k][w, j]]
-                parts.append(jnp.concatenate(rows, axis=0))
-        return jnp.concatenate(parts, axis=1)
-
-    def dot_n(n, stx, sty, stzs):
-        blocks = []
-        lhs = lhs_of(stx, sty, stzs)
-        two_sided = isinstance(stx, tuple)
-        if two_sided:
-            side = stx[1]
-            stx = 2 * side
-        for stz in stzs:
-            mains = []
-            tails = []
-            for s in range(8):
+            rows = []
+            lasts = []
+            for s in order:
                 sx, sy, sz = s >> 2, (s >> 1) & 1, s & 1
                 pair = []
-                for h in range(2):
-                    if n < 4:
-                        c = 2 * n + h
-                        kx = 2 * stx + sx - (c >> 2) + 1
+                for c in cs:
+                    if c < 8:
+                        kx = 2 * step_x + sx - (c >> 2) + 1
                         ky = 2 * sty + sy - ((c >> 1) & 1) + 1
                         kz = 2 * stz + sz - (c & 1) + 1
                         pair.append((tm[kx, ky, kz, 0:MAIN, :], tm[kx, ky, kz, MAIN:ROWS, :]))
                     else:
-                        k = ((2 * stx + sx - h + 1) * 6 + 2 * sty + sy) * 6 + 2 * stz + sz
+                        k = ((2 * step_x + sx - (c - 8) + 1) * 6 + 2 * sty + sy) * 6 + 2 * stz + sz
                         pair.append((v[k, 0:MAIN, :], v[k, MAIN:ROWS, :]))
-                mains.append(jnp.concatenate([p[0] for p in pair], axis=1))
-                tails.append(jnp.concatenate([p[1] for p in pair], axis=1))
-            blocks += mains + tails
+                rows.append(jnp.concatenate([p[0] for p in pair], axis=1))
+                lasts.append(jnp.concatenate([p[1] for p in pair], axis=1))
+            for a in range(0, 8, 2):
+                fixed = isinstance(sty, int) and not two_sided and cs[0] < 8
+                if fixed and all(
+                    near((stx, sty, stz), s, c) for s in order[a : a + 2] for c in cs
+                ):
+                    continue
+                parts += [lhs_part(stx, w, order[a]), lhs_part(stx, w, order[a + 1])]
+                blocks += rows[a : a + 2]
+            parts += [lhs_part(stx, w, 8), lhs_part(stx, w, 9)]
+            blocks += [lasts[order.index(s)] for s in range(8)]
+        lhs = jnp.concatenate(parts, axis=1)
         rhs = jnp.concatenate(blocks, axis=0)
         res = jnp.dot(lhs, rhs, preferred_element_type=F32)
-        for h in range(2):
+        for h, c in enumerate(cs):
             own = res[:, MAIN * h : MAIN * (h + 1)]
             if two_sided:
-                acc[2 * n + h, pl.ds(pl.multiple_of(96 * side, 32), 32)] += own[0:32]
-                acc[2 * n + h, pl.ds(pl.multiple_of(32 - 32 * side, 32), 96)] += own[32:128]
-                acc[2 * n + h, 128:160] += own[128:160]
+                side = stx[1]
+                acc[c, pl.ds(pl.multiple_of(96 * side, 32), 32)] += own[0:32]
+                acc[c, pl.ds(pl.multiple_of(32 - 32 * side, 32), 96)] += own[32:128]
+                acc[c, 128:160] += own[128:160]
             else:
-                acc[2 * n + h] += own
+                acc[c] += own
 
     def block(stx, sty, stzs, fill):
+        centre = stx == 1 and isinstance(sty, int) and sty == 1
         for n in range(4):
-            dot_n(n, stx, sty, stzs)
+            if centre:
+                first = 4 * (n >> 1) + (n & 1)
+                dot_n((first, first + 2), stx, sty, stzs, (0, 2, 4, 6, 1, 3, 5, 7))
+            else:
+                dot_n((2 * n, 2 * n + 1), stx, sty, stzs)
             for k in range(n * len(fill) // 4, (n + 1) * len(fill) // 4):
                 fill[k]()
 
@@ -470,13 +482,13 @@
         wait_t(2, 4)
     with jax.named_scope("mxu1"):
 
-        def body(i, _):
+        for i in range(2):
             units = [lambda q=q: tail_unit(2, 3 * i + q) for q in range(3)]
             units.append(lambda: tail_unit(4, i))
-            block(1, 2 * i, (0, 1, 2), units)
-            return 0
-
-        lax.fori_loop(0, 2, body, 0)
+
+            @pl.when(lev >= 0)
+            def _():
+                block(1, 2 * i, (0, 1, 2), units)
 
     @pl.when((col < n_col - 1) & (lev == 1))
     def _():
@@ -493,7 +505,7 @@
 
     def tail_dots(stx):
         def body(sty, _):
-            dot_n(4, stx, sty, (0, 1, 2))
+            dot_n((8, 9), stx, sty, (0, 1, 2))
             return 0
 
         with jax.named_scope("mxu_tail"):

time: 34.3 us -> 35.1 us (1.023)
  Pallas kernels: 33.8 us -> 34.6 us
    pallas_call x1, Pallas kernels: 31.6 us -> 32.4 us  [shards(): pl.pallas_call(kernel, out_shape=pltpu.VMEM((NBLK, 160, MAIN), F32), in_s...]
where the time goes in v6:
time: 35.1 us; the launch traced here: 34.8 us
  Pallas kernels  34.6 us (99%)
    pallas_call x1, Pallas kernels, shards(): pl.pallas_call(kernel, out_shape=pltpu.VMEM((NBLK, 160, MAIN), F32), in_s...  32.4 us
    pallas_call x1, Pallas kernels, shards(): pl.pallas_call(finish, out_shape=jax.ShapeDtypeStruct((8, 8, 16, CH), F32...  2.19 us

profile of v6, /device:TPU:6, one launch (start us, length us, event | category | flops | bytes accessed | tf_op | source)
XLA Modules:
  0.0 34.8 jit_solution(4858879416860857763)
XLA Ops:
  0.0 0.0 copy-start
  0.0 32.4 %downward.1.acc = f32[10,160,128]{2,1,0:T(8,128)S(1)} custom-call(bf16[8,16,16,152]{3,2,1,0:T(8,128)(2,1)} %mf.1, bf16[4,8,8,152]{3,2,1,0:T(8,128)(2,1)} %mm.1, bf16[2,4,4,152]{3,2,1,0:T(4,128)(2,1)} %mc.1, bf16[1,2,2,152]{3,2,1,0:T(2,128)(2,1)} %mt.1, bf16[7,7,7,152,152]{4,3,2,1,0:T(8,128)(2,1)} %tr.1), custom_call_target="tpu_custom_call" | custom-call | tf_op jit(solution)/shard_map/downward/pallas_call | solution.py:738
  32.4 0.0 copy-done
  32.4 2.2 %upsample.1 = f32[8,8,16,152]{3,2,1,0:T(8,128)} custom-call(f32[10,160,128]{2,1,0:T(8,128)S(1)} %downward.1.acc, bf16[2,2,2,152,152]{4,3,2,1,0:T(8,128)(2,1)S(1)} %copy-done), custom_call_target="tpu_custom_call" | custom-call | tf_op jit(solution)/shard_map/upsample/pallas_call | solution.py:775
Async XLA Ops:
  0.0 32.4 %copy-start = (bf16[2,2,2,152,152]{4,3,2,1,0:T(8,128)(2,1)S(1)}, bf16[2,2,2,152,152]{4,3,2,1,0:T(8,128)(2,1)}, u32[]{:S(2)}) copy-start(bf16[2,2,2,152,152]{4,3,2,1,0:T(8,128)(2,1)} %up.1) | copy-start | bytes 1108996
